TPU v7x, 32 devices: a whole 2x2x4 slice. The times are simulated.
32 devices in a mesh: groups: 2 (over y), cell: 4 (over z), wall: 4 (over x, core).
Axes of the slice: x: 2, y: 2, z: 4, core: 2. Of those that a mesh axis runs over, the one named last changes fastest.
Arguments:
- mem_pos: float32 [3, 2048], P(None, ('groups', 'cell')), parts along dimension 1, may hold values from -0.7 to 8, as said below
- forces: bfloat16 [32, 3, 2048], P(None, None, ('groups', 'cell', 'wall')), parts along dimension 2, may hold values from -1.59375 to 1.59375
- wall_pos: float32 [3, 1024], P(None, ('groups', 'wall')), parts along dimension 1, may hold values from -1 to 8, as said below
- wall_normal: float32 [3, 1024], P(None, ('groups', 'wall')), parts along dimension 1, as said below
- wall_data: float32 [32, 3, 1024], P(None, None, ('groups', 'wall')), parts along dimension 2, may hold values from -6 to 6
- lag_density: bfloat16 [16, 3, 1024], P(None, None, ('groups', 'wall', 'cell')), parts along dimension 2, may hold values from -15 to 15
- batch_order: int32 [32], replicated, may hold values from 0 to 31, each once
Outputs:
- membrane_velocity: float32 [32, 3, 2048], P(None, None, ('groups', 'cell', 'wall')), parts along dimension 2
- wall_density: float32 [16, 3, 1024], P(None, None, ('groups', 'wall', 'cell')), parts along dimension 2
There are 2 independent parts, one for each index of `groups`. A program takes and returns all parts, laid end to end along the dimension named above; an argument that names none is the same for every part. Nothing has to cross between parts.
Inputs may be any that keep to these rules, and one draw needn't show every extreme that they name: `mem_pos`: each membrane point lies within 0.7 of the vessel axis (first two coordinates) with third coordinate between 0 and 8. `wall_pos`: each wall point lies on the unit cylinder around the vessel axis, third coordinate between 0 and 8. `wall_normal`: column w is the outward unit normal of the cylinder at wall_pos[:, w] times 16 pi / 512.
All inputs are finite; a program needn't handle non-finite values.
Results may differ from a plain program's by a relative error of at most 0.002.
Values may be sent and summed in bfloat16 or wider, within the bound.
A program may use at most 64 MiB of HBM per device.

v0:
```python
import functools
import math

import jax
import jax.numpy as jnp
from jax import lax
from jax.experimental import pallas as pl
from jax.experimental.pallas import tpu as pltpu
from jax.sharding import PartitionSpec as P

stokes_coef = 1.0 / (8.0 * math.pi)


def single_tile(targets, sources):
    separation = targets[:, None, :] - sources[:, :, None]
    inverse = lax.rsqrt(jnp.sum(separation * separation, axis=0))
    inverse_cube = inverse * inverse * inverse
    stacked = []
    for second_dim in range(3):
        entries_row = []
        for first_dim in range(3):
            element = separation[first_dim] * separation[second_dim] * inverse_cube
            if first_dim == second_dim:
                element = element + inverse
            entries_row.append(element * stokes_coef)
        stacked.append(jnp.stack(entries_row, axis=1))
    kernel_tile = jnp.stack(stacked, axis=0)
    return kernel_tile.reshape(3 * sources.shape[1], 3 * targets.shape[1]).astype(jnp.bfloat16)


def double_tile(targets, sources, normals):
    separation = targets[:, None, :] - sources[:, :, None]
    inverse = lax.rsqrt(jnp.sum(separation * separation, axis=0))
    normal_flux = jnp.sum(separation * normals[:, :, None], axis=0)
    weight = -6.0 * stokes_coef * normal_flux * inverse**5
    stacked = []
    for second_dim in range(3):
        entries_row = []
        for first_dim in range(3):
            entries_row.append(weight * separation[first_dim] * separation[second_dim])
        stacked.append(jnp.stack(entries_row, axis=1))
    kernel_tile = jnp.stack(stacked, axis=0)
    return kernel_tile.reshape(3 * sources.shape[1], 3 * targets.shape[1]).astype(jnp.bfloat16)


def shards(mem_pos, forces, wall_pos, wall_normal, wall_data, lag_density, batch_order):
    columns = forces.shape[0]
    halfway = columns // 2
    point_count = mem_pos.shape[1]
    wall_count = wall_pos.shape[1]
    shard_width = lag_density.shape[2]
    piece_len = math.gcd(point_count, 128)
    block_count = point_count // piece_len
    first_rows = batch_order[:halfway]
    second_rows = batch_order[halfway:]
    force_block = lax.all_gather(forces, "wall", axis=2, tiled=True)
    lag_block = lax.all_gather(lag_density, "cell", axis=2, tiled=True)
    lag_flat = lag_block.reshape(halfway, 3 * wall_count)

    def position_at(block_index):
        return lax.dynamic_slice_in_dim(mem_pos, block_index * piece_len, piece_len, 1)

    def single_term(block_index):
        loaded = lax.dynamic_slice_in_dim(force_block, block_index * piece_len, piece_len, 2)
        loaded = loaded.reshape(columns, 3 * piece_len)
        return jnp.dot(
            loaded,
            single_tile(wall_pos, position_at(block_index)),
            preferred_element_type=jnp.float32,
        )

    def double_term(dense_rows, block_index):
        kernel_tile = double_tile(position_at(block_index), wall_pos, wall_normal)
        product = jnp.dot(dense_rows, kernel_tile, preferred_element_type=jnp.float32)
        return product.reshape(dense_rows.shape[0], 3, piece_len)

    def place_block(target, piece, block_index):
        return lax.dynamic_update_slice_in_dim(target, piece, block_index * piece_len, 2)

    empty_wall = jnp.zeros((columns, 3 * wall_count), jnp.float32)

    def add_single(block_index, running):
        return running + single_term(block_index)

    running = lax.fori_loop(0, block_count, add_single, empty_wall)
    wall_term = running.reshape(columns, 3, wall_count)
    position_cell = lax.axis_index("cell")
    first_sum = lax.psum(jnp.take(wall_term, first_rows, axis=0), "cell")
    first_block = (2.0 * (jnp.take(wall_data, first_rows, axis=0) - first_sum)).astype(jnp.bfloat16)
    second_sum = lax.psum_scatter(
        jnp.take(wall_term, second_rows, axis=0).astype(jnp.bfloat16),
        "cell",
        scatter_dimension=2,
        tiled=True,
    ).astype(jnp.float32)
    second_data = lax.dynamic_slice_in_dim(
        jnp.take(wall_data, second_rows, axis=0), position_cell * shard_width, shard_width, 2
    )
    wall_density = 2.0 * (second_data - second_sum)
    first_flat = first_block.reshape(halfway, 3 * wall_count)
    carried = jnp.concatenate([lag_flat, first_flat], axis=0)

    def all_terms(block_index, target):
        return place_block(target, double_term(carried, block_index), block_index)

    membrane_term = lax.fori_loop(
        0, block_count, all_terms, jnp.zeros((columns, 3, point_count), jnp.float32)
    )
    batched = lax.psum_scatter(membrane_term, "wall", scatter_dimension=2, tiled=True)
    membrane_velocity = jnp.zeros_like(batched).at[batch_order].set(batched)
    return (membrane_velocity, wall_density)

LANES = 128
MESH = pl.DeviceIdType.MESH
NT = (((1,), (1,)), ((), ()))


def nearest(position, rank, count):
    mirrored = position >= (count + 1) // 2
    here = jnp.where(mirrored, count - 1 - position, position)
    other = jnp.where(rank <= here, rank - 1, rank)
    return jnp.where(mirrored, count - 1 - other, other)


def fused_kernel(
    cells,
    walls,
    mem_hbm,
    force_hbm,
    wall_hbm,
    normal_hbm,
    data_hbm,
    lag_hbm,
    order_hbm,
    out_ref,
    density_ref,
    force_ref,
    data_ref,
    lag_ref,
    order_ref,
    blocks,
    mem_all,
    wall_all,
    first_all,
    wall_cols,
    mem_cols,
    single_all,
    double_all,
    load_sem,
    block_send,
    block_recv,
    forward_send,
    mem_send,
    mem_recv,
    pos_send,
    pos_recv,
    first_send,
    first_recv,
):
    cell = lax.axis_index("cell")
    wall = lax.axis_index("wall")
    columns = order_ref.shape[1]
    halfway = columns // 2
    point_count = mem_hbm.shape[1]
    wall_count = wall_hbm.shape[1]
    own_points = force_ref.shape[2]
    shard_width = lag_ref.shape[2]

    loads = [
        pltpu.make_async_copy(given, held, load_sem.at[at])
        for at, (given, held) in enumerate(
            (
                (order_hbm, order_ref),
                (force_hbm, force_ref),
                (lag_hbm, lag_ref),
                (mem_hbm, mem_all.at[cell]),
                (wall_hbm, wall_all.at[wall, 0]),
                (normal_hbm, wall_all.at[wall, 1]),
                (data_hbm, data_ref),
            )
        )
    ]
    for load in loads:
        load.start()

    cell_peers = [lax.rem(cell + step, cells) for step in range(1, cells)]
    wall_peers = [lax.rem(wall + step, walls) for step in range(1, walls)]

    barrier = pltpu.get_barrier_semaphore()
    for peer in cell_peers:
        pl.semaphore_signal(barrier, inc=1, device_id={"cell": peer}, device_id_type=MESH)
    for peer in wall_peers:
        pl.semaphore_signal(barrier, inc=1, device_id={"wall": peer}, device_id_type=MESH)

    loads[0].wait()
    order_row = order_ref[...]
    row_ids = lax.broadcasted_iota(jnp.int32, (columns, columns), 0)
    col_ids = lax.broadcasted_iota(jnp.int32, (columns, columns), 1)
    scatter = (row_ids == order_row).astype(jnp.float32).astype(jnp.bfloat16)
    unit = (row_ids == col_ids).astype(jnp.float32).astype(jnp.bfloat16)
    gather_f32 = lax.dot_general(unit, scatter, NT, preferred_element_type=jnp.float32)
    gather = gather_f32.astype(jnp.bfloat16)

    loads[1].wait()
    rows = [jnp.dot(gather, force_ref[j], preferred_element_type=jnp.float32) for j in range(3)]
    loads[2].wait()
    lag_rows = [lag_ref[j].astype(jnp.float32) for j in range(3)]
    spare = jnp.zeros((halfway, own_points - 2 * shard_width), jnp.float32)
    unused = jnp.zeros((halfway, own_points - shard_width), jnp.float32)
    halves = (
        ([row[:halfway] for row in rows], (lag_rows[0], lag_rows[1], spare)),
        ([row[halfway:] for row in rows], (lag_rows[2], unused)),
    )
    for wave, (part, rest) in enumerate(halves):
        rest = [piece for piece in rest if piece.shape[1]]
        pair = jnp.concatenate([part[0], part[1]], axis=1)
        blocks[wave, cell, wall, 0] = pair.astype(jnp.bfloat16)
        pair = jnp.concatenate([part[2], *rest], axis=1)
        blocks[wave, cell, wall, 1] = pair.astype(jnp.bfloat16)
    for load in loads[3:6]:
        load.wait()

    def block_copy(wave, source, to_cell, rank):
        return pltpu.make_async_remote_copy(
            blocks.at[wave, source, wall],
            blocks.at[wave, source, wall],
            block_send.at[wave, rank],
            block_recv.at[wave, source, wall],
            device_id={"cell": to_cell},
            device_id_type=MESH,
        )

    def forward_copy(wave, source_cell, source_wall, to_wall, rank, slot):
        return pltpu.make_async_remote_copy(
            blocks.at[wave, source_cell, source_wall],
            blocks.at[wave, source_cell, source_wall],
            forward_send.at[wave, rank, slot],
            block_recv.at[wave, source_cell, source_wall],
            device_id={"wall": to_wall},
            device_id_type=MESH,
        )

    def mem_copy(source, to_cell, rank):
        return pltpu.make_async_remote_copy(
            mem_all.at[source],
            mem_all.at[source],
            mem_send.at[rank],
            mem_recv.at[source],
            device_id={"cell": to_cell},
            device_id_type=MESH,
        )

    def pos_copy(source, to_wall, rank):
        return pltpu.make_async_remote_copy(
            wall_all.at[source],
            wall_all.at[source],
            pos_send.at[rank],
            pos_recv.at[source],
            device_id={"wall": to_wall},
            device_id_type=MESH,
        )

    def first_copy(source, to_wall, rank):
        return pltpu.make_async_remote_copy(
            first_all.at[source],
            first_all.at[source],
            first_send.at[rank],
            first_recv.at[source],
            device_id={"wall": to_wall},
            device_id_type=MESH,
        )

    pl.semaphore_wait(barrier, cells + walls - 2)

    sent = []

    def send(copy):
        sent.append(copy)
        copy.start()

    def send_own(wave):
        for rank in range(cells - 1):
            send(block_copy(wave, cell, nearest(cell, cells - 1 - rank, cells), rank))
        for slot, peer in enumerate(wall_peers):
            send(forward_copy(wave, cell, wall, peer, 0, slot))

    def pass_on(wave, rank):
        source = nearest(cell, rank, cells)
        block_copy(wave, source, source, 0).wait_recv()
        for slot, peer in enumerate(wall_peers):
            send(forward_copy(wave, source, wall, peer, rank, slot))

    send_own(0)
    for rank, peer in enumerate(cell_peers):
        send(mem_copy(cell, peer, rank))
    for rank, peer in enumerate(wall_peers):
        send(pos_copy(wall, peer, rank))
    send_own(1)

    for j in range(3):
        wall_cols[j] = jnp.broadcast_to(wall_all[wall, 0, j : j + 1, :], (LANES, wall_count)).T
        mem_cols[j] = jnp.broadcast_to(mem_all[cell, j : j + 1, :], (LANES, point_count)).T
    loads[6].wait()

    def fill_single(source):
        for start in range(0, point_count, LANES):
            apart = [
                wall_cols[j] - mem_all[source, j : j + 1, start : start + LANES] for j in range(3)
            ]
            square = apart[0] * apart[0] + apart[1] * apart[1] + apart[2] * apart[2]
            inverse = lax.rsqrt(square)
            scaled = stokes_coef * inverse
            cube = scaled * (inverse * inverse)
            for j in range(3):
                along = apart[j] * cube
                for i in range(j + 1):
                    element = along * apart[i]
                    if i == j:
                        element = element + scaled
                    element = element.astype(jnp.bfloat16)
                    for a, b in {(i, j), (j, i)}:
                        single_all[
                            source,
                            a * wall_count : (a + 1) * wall_count,
                            b * point_count + start : b * point_count + start + LANES,
                        ] = element

    def fill_double(source):
        own = pl.ds(pl.multiple_of(wall * own_points, own_points), own_points)
        for start in range(0, wall_count, LANES):
            apart = [
                mem_cols[j, own, :] - wall_all[source, 0, j : j + 1, start : start + LANES]
                for j in range(3)
            ]
            square = apart[0] * apart[0] + apart[1] * apart[1] + apart[2] * apart[2]
            inverse = lax.rsqrt(square)
            flux = (
                apart[0] * wall_all[source, 1, 0:1, start : start + LANES]
                + apart[1] * wall_all[source, 1, 1:2, start : start + LANES]
                + apart[2] * wall_all[source, 1, 2:3, start : start + LANES]
            )
            inverse_square = inverse * inverse
            fifth = inverse_square * inverse_square * inverse
            weight = (-6.0 * stokes_coef) * flux * fifth
            for j in range(3):
                along = apart[j] * weight
                for i in range(j + 1):
                    element = (along * apart[i]).astype(jnp.bfloat16)
                    for a, b in {(i, j), (j, i)}:
                        double_all[
                            source,
                            a * own_points : (a + 1) * own_points,
                            b * wall_count + start : b * wall_count + start + LANES,
                        ] = element

    fill_single(cell)
    fill_double(wall)
    data_rows = [
        jnp.dot(gather_f32, data_ref[j], precision=lax.Precision.HIGHEST) for j in range(3)
    ]

    for rank in range(1, cells):
        pass_on(0, rank)
    for rank in range(1, cells):
        source = nearest(cell, rank, cells)
        mem_copy(source, source, 0).wait_recv()
        fill_single(source)
    for rank in range(1, cells):
        pass_on(1, rank)

    def single_layer(wave):
        velocity = jnp.zeros((halfway, 3 * wall_count), jnp.float32)
        for rank in range(cells):
            source = cell if rank == 0 else nearest(cell, rank, cells)
            for peer in wall_peers:
                forward_copy(wave, source, peer, peer, 0, 0).wait_recv()
            pairs = [blocks[wave, source, k, 0] for k in range(walls)]
            thirds = [blocks[wave, source, k, 1] for k in range(walls)]
            loaded = [piece[:, :own_points] for piece in pairs]
            loaded += [piece[:, own_points:] for piece in pairs]
            loaded += [piece[:, :own_points] for piece in thirds]
            velocity = velocity + lax.dot_general(
                jnp.concatenate(loaded, axis=1),
                single_all[source],
                NT,
                preferred_element_type=jnp.float32,
            )
        held = slice(wave * halfway, (wave + 1) * halfway)
        return [
            2.0 * (data_rows[j][held] - velocity[:, j * wall_count : (j + 1) * wall_count])
            for j in range(3)
        ]

    first_rows = single_layer(0)
    for j in range(3):
        first_all[wall, j] = first_rows[j].astype(jnp.bfloat16)
    for rank, peer in enumerate(wall_peers):
        send(first_copy(wall, peer, rank))

    for peer in wall_peers:
        pos_copy(peer, peer, 0).wait_recv()
        fill_double(peer)
    shift = lax.rem((cells - cell) * shard_width, wall_count)
    second_rows = single_layer(1)
    for j in range(3):
        density_ref[j] = pltpu.roll(second_rows[j], shift, 1)[:, :shard_width]

    lag_places = ((0, own_points), (0, own_points + shard_width), (1, own_points))
    total = jnp.zeros((columns, 3 * own_points), jnp.float32)
    for source in range(walls):
        lag = jnp.concatenate(
            [
                blocks[wave, k, source, 1, :, start : start + shard_width]
                for wave, start in lag_places
                for k in range(cells)
            ],
            axis=1,
        )
        placed = jnp.dot(scatter[:, :halfway], lag, preferred_element_type=jnp.float32)
        total = total + lax.dot_general(
            placed.astype(jnp.bfloat16), double_all[source], NT, preferred_element_type=jnp.float32
        )

    last = len(sent) - (walls - 1)
    for copy in sent[:last]:
        copy.wait_send()

    for rank in range(walls):
        source = wall
        if rank:
            source = wall_peers[rank - 1]
            first_copy(source, source, 0).wait_recv()
        first = jnp.concatenate([first_all[source, j] for j in range(3)], axis=1)
        placed = jnp.dot(scatter[:, halfway:], first, preferred_element_type=jnp.float32)
        total = total + lax.dot_general(
            placed.astype(jnp.bfloat16), double_all[source], NT, preferred_element_type=jnp.float32
        )
    for i in range(3):
        out_ref[i] = total[:, i * own_points : (i + 1) * own_points]

    for copy in sent[last:]:
        copy.wait_send()


def write_kernel(velocity_ref, density_ref, velocity_hbm, density_hbm, sem):
    first = pltpu.make_async_copy(velocity_ref, velocity_hbm, sem.at[0])
    second = pltpu.make_async_copy(density_ref, density_hbm, sem.at[1])
    first.start()
    second.start()
    first.wait()
    second.wait()


def fused_shards(cells, walls, mem_pos, forces, wall_pos, wall_normal, wall_data, lag_density, batch_order):
    columns = forces.shape[0]
    halfway = columns // 2
    point_count = mem_pos.shape[1]
    wall_count = wall_pos.shape[1]
    own_points = forces.shape[2]
    shard_width = lag_density.shape[2]
    dma = pltpu.SemaphoreType.DMA
    vmem = pl.BlockSpec(memory_space=pltpu.VMEM)
    hbm = pl.BlockSpec(memory_space=pltpu.HBM)
    velocity, density = pl.pallas_call(
        functools.partial(fused_kernel, cells, walls),
        out_shape=(
            pltpu.VMEM((3, columns, own_points), jnp.float32),
            pltpu.VMEM((3, halfway, shard_width), jnp.float32),
        ),
        in_specs=[hbm] * 7,
        out_specs=(vmem, vmem),
        scratch_shapes=[
            pltpu.VMEM((3, columns, own_points), jnp.bfloat16),
            pltpu.VMEM((3, columns, wall_count), jnp.float32),
            pltpu.VMEM((3, halfway, shard_width), jnp.bfloat16),
            pltpu.VMEM((1, columns), jnp.int32),
            pltpu.VMEM((2, cells, walls, 2, halfway, 2 * own_points), jnp.bfloat16),
            pltpu.VMEM((cells, 3, point_count), jnp.float32),
            pltpu.VMEM((walls, 2, 3, wall_count), jnp.float32),
            pltpu.VMEM((walls, 3, halfway, wall_count), jnp.bfloat16),
            pltpu.VMEM((3, wall_count, LANES), jnp.float32),
            pltpu.VMEM((3, point_count, LANES), jnp.float32),
            pltpu.VMEM((cells, 3 * wall_count, 3 * point_count), jnp.bfloat16),
            pltpu.VMEM((walls, 3 * own_points, 3 * wall_count), jnp.bfloat16),
            dma((7,)),
            dma((2, cells - 1)),
            dma((2, cells, walls)),
            dma((2, cells, walls - 1)),
            dma((cells - 1,)),
            dma((cells,)),
            dma((walls - 1,)),
            dma((walls,)),
            dma((walls - 1,)),
            dma((walls,)),
        ],
        compiler_params=pltpu.CompilerParams(
            collective_id=0, has_side_effects=True, vmem_limit_bytes=VMEM_GRANT
        ),
        name="coupling",
    )(
        mem_pos,
        jnp.transpose(forces, (1, 0, 2)),
        wall_pos,
        wall_normal,
        jnp.transpose(wall_data, (1, 0, 2)),
        jnp.transpose(lag_density, (1, 0, 2)),
        batch_order.reshape(1, columns),
    )
    velocity, density = pl.pallas_call(
        write_kernel,
        out_shape=(
            jax.ShapeDtypeStruct(velocity.shape, velocity.dtype),
            jax.ShapeDtypeStruct(density.shape, density.dtype),
        ),
        in_specs=[vmem] * 2,
        out_specs=(hbm, hbm),
        scratch_shapes=[dma((2,))],
        compiler_params=pltpu.CompilerParams(vmem_limit_bytes=1024 * 1024),
        name="write",
    )(velocity, density)
    return (jnp.transpose(velocity, (1, 0, 2)), jnp.transpose(density, (1, 0, 2)))


VMEM_GRANT = 60 * 1024 * 1024


def step(cells, walls, mem_pos, forces, wall_pos, *rest):
    point_count = mem_pos.shape[1]
    wall_count = wall_pos.shape[1]
    own_points = forces.shape[2]
    shard_width = rest[2].shape[2]
    tiles = 18 * wall_count * (cells * point_count + walls * own_points)
    fits = tiles <= VMEM_GRANT // 2
    aligned = (
        point_count % LANES == 0
        and wall_count % LANES == 0
        and 2 * own_points == LANES
        and 2 * shard_width <= own_points
    )
    if fits and aligned:
        return fused_shards(cells, walls, mem_pos, forces, wall_pos, *rest)
    return shards(mem_pos, forces, wall_pos, *rest)


def solution(mesh):
    placed = (
        P(None, ("groups", "cell")),
        P(None, None, ("groups", "cell", "wall")),
        P(None, ("groups", "wall")),
        P(None, ("groups", "wall")),
        P(None, None, ("groups", "wall")),
        P(None, None, ("groups", "wall", "cell")),
        P(),
    )
    return jax.shard_map(
        functools.partial(step, mesh.shape["cell"], mesh.shape["wall"]),
        mesh=mesh,
        in_specs=placed,
        out_specs=(
            P(None, None, ("groups", "cell", "wall")),
            P(None, None, ("groups", "wall", "cell")),
        ),
        check_vma=False,
    )
```

profile of v0, /device:TPU:0, one launch (start us, length us, event | category | flops | bytes accessed | tf_op | source)
XLA Modules:
  0.0 16.6 jit_solution(854244761908114184)
XLA Ops:
  0.6 15.4 %coupling.1 = (f32[3,32,64]{2,1,0:T(8,128)S(1)}, f32[3,16,32]{2,1,0:T(8,128)S(1)}) custom-call(f32[3,256]{1,0:T(4,128)} %mem_hbm.1, bf16[3,32,64]{2,1,0:T(8,128)(2,1)} %bitcast.7, f32[3,128]{1,0:T(4,128)} %wall_hbm.1, f32[3,128]{1,0:T(4,128)} %normal_hbm.1, f32[3,32,128]{2,1,0:T(8,128)} %bitcast.6, bf16[3,16,32]{2,1,0:T(8,128)(2,1)} %bitcast.8, s32[1,32]{1,0:T(1,128)} %bitcast.9), custom_call_target="tpu_custom_call" | custom-call | tf_op jit(solution)/shard_map/coupling/pallas_call | solution.py:464
  16.0 0.6 %write.1 = (f32[3,32,64]{2,1,0:T(8,128)}, f32[3,16,32]{2,1,0:T(8,128)}) custom-call(f32[3,32,64]{2,1,0:T(8,128)S(1)} %get-tuple-element.6.velocity_ref, f32[3,16,32]{2,1,0:T(8,128)S(1)} %get-tuple-element.7.density_ref), custom_call_target="tpu_custom_call" | custom-call | tf_op jit(solution)/shard_map/write/pallas_call | solution.py:509
where the time goes:
time: 16.8 us; the launch traced here: 16.6 us
  Pallas kernels  16 us (95%)
  between operations  0.64 us (4%)
    pallas_call x1, Pallas kernels, fused_shards(): pl.pallas_call(functools.partial(fused_kernel, cells, walls), out_shape=(...  15.4 us
    pallas_call x1, Pallas kernels, fused_shards(): pl.pallas_call(write_kernel, out_shape=(jax.ShapeDtypeStruct(velocity.sha...  0.64 us

commit v1 on v0

v1 whole, which is shorter than its diff:
```python
import functools
import math

import jax
import jax.numpy as jnp
from jax import lax
from jax.experimental import pallas as pl
from jax.experimental.pallas import tpu as pltpu
from jax.sharding import PartitionSpec as P

stokes_coef = 1.0 / (8.0 * math.pi)


def single_tile(targets, sources):
    separation = targets[:, None, :] - sources[:, :, None]
    inverse = lax.rsqrt(jnp.sum(separation * separation, axis=0))
    inverse_cube = inverse * inverse * inverse
    stacked = []
    for second_dim in range(3):
        entries_row = []
        for first_dim in range(3):
            element = separation[first_dim] * separation[second_dim] * inverse_cube
            if first_dim == second_dim:
                element = element + inverse
            entries_row.append(element * stokes_coef)
        stacked.append(jnp.stack(entries_row, axis=1))
    kernel_tile = jnp.stack(stacked, axis=0)
    return kernel_tile.reshape(3 * sources.shape[1], 3 * targets.shape[1]).astype(jnp.bfloat16)


def double_tile(targets, sources, normals):
    separation = targets[:, None, :] - sources[:, :, None]
    inverse = lax.rsqrt(jnp.sum(separation * separation, axis=0))
    normal_flux = jnp.sum(separation * normals[:, :, None], axis=0)
    weight = -6.0 * stokes_coef * normal_flux * inverse**5
    stacked = []
    for second_dim in range(3):
        entries_row = []
        for first_dim in range(3):
            entries_row.append(weight * separation[first_dim] * separation[second_dim])
        stacked.append(jnp.stack(entries_row, axis=1))
    kernel_tile = jnp.stack(stacked, axis=0)
    return kernel_tile.reshape(3 * sources.shape[1], 3 * targets.shape[1]).astype(jnp.bfloat16)


def shards(mem_pos, forces, wall_pos, wall_normal, wall_data, lag_density, batch_order):
    columns = forces.shape[0]
    halfway = columns // 2
    point_count = mem_pos.shape[1]
    wall_count = wall_pos.shape[1]
    shard_width = lag_density.shape[2]
    piece_len = math.gcd(point_count, 128)
    block_count = point_count // piece_len
    first_rows = batch_order[:halfway]
    second_rows = batch_order[halfway:]
    force_block = lax.all_gather(forces, "wall", axis=2, tiled=True)
    lag_block = lax.all_gather(lag_density, "cell", axis=2, tiled=True)
    lag_flat = lag_block.reshape(halfway, 3 * wall_count)

    def position_at(block_index):
        return lax.dynamic_slice_in_dim(mem_pos, block_index * piece_len, piece_len, 1)

    def single_term(block_index):
        loaded = lax.dynamic_slice_in_dim(force_block, block_index * piece_len, piece_len, 2)
        loaded = loaded.reshape(columns, 3 * piece_len)
        return jnp.dot(
            loaded,
            single_tile(wall_pos, position_at(block_index)),
            preferred_element_type=jnp.float32,
        )

    def double_term(dense_rows, block_index):
        kernel_tile = double_tile(position_at(block_index), wall_pos, wall_normal)
        product = jnp.dot(dense_rows, kernel_tile, preferred_element_type=jnp.float32)
        return product.reshape(dense_rows.shape[0], 3, piece_len)

    def place_block(target, piece, block_index):
        return lax.dynamic_update_slice_in_dim(target, piece, block_index * piece_len, 2)

    empty_wall = jnp.zeros((columns, 3 * wall_count), jnp.float32)

    def add_single(block_index, running):
        return running + single_term(block_index)

    running = lax.fori_loop(0, block_count, add_single, empty_wall)
    wall_term = running.reshape(columns, 3, wall_count)
    position_cell = lax.axis_index("cell")
    first_sum = lax.psum(jnp.take(wall_term, first_rows, axis=0), "cell")
    first_block = (2.0 * (jnp.take(wall_data, first_rows, axis=0) - first_sum)).astype(jnp.bfloat16)
    second_sum = lax.psum_scatter(
        jnp.take(wall_term, second_rows, axis=0).astype(jnp.bfloat16),
        "cell",
        scatter_dimension=2,
        tiled=True,
    ).astype(jnp.float32)
    second_data = lax.dynamic_slice_in_dim(
        jnp.take(wall_data, second_rows, axis=0), position_cell * shard_width, shard_width, 2
    )
    wall_density = 2.0 * (second_data - second_sum)
    first_flat = first_block.reshape(halfway, 3 * wall_count)
    carried = jnp.concatenate([lag_flat, first_flat], axis=0)

    def all_terms(block_index, target):
        return place_block(target, double_term(carried, block_index), block_index)

    membrane_term = lax.fori_loop(
        0, block_count, all_terms, jnp.zeros((columns, 3, point_count), jnp.float32)
    )
    batched = lax.psum_scatter(membrane_term, "wall", scatter_dimension=2, tiled=True)
    membrane_velocity = jnp.zeros_like(batched).at[batch_order].set(batched)
    return (membrane_velocity, wall_density)

LANES = 128
MESH = pl.DeviceIdType.MESH
NT = (((1,), (1,)), ((), ()))


def fused_kernel(
    cells,
    walls,
    mem_hbm,
    force_hbm,
    wall_hbm,
    normal_hbm,
    data_hbm,
    lag_hbm,
    order_hbm,
    out_ref,
    density_ref,
    order_ref,
    force_all,
    lag_all,
    mem_all,
    wall_all,
    data_all,
    wall_cols,
    mem_cols,
    single_all,
    double_all,
    part_mine,
    part_other,
    load_sem,
    force_send,
    force_recv,
    lag_send,
    lag_recv,
    mem_send,
    mem_recv,
    wall_send,
    wall_recv,
    data_send,
    data_recv,
    part_send,
    part_recv,
    ready,
):
    cell = lax.axis_index("cell")
    wall = lax.axis_index("wall")
    chip = wall // 2
    core = wall % 2
    other_core = 1 - core
    other_chip = 1 - chip
    columns = order_ref.shape[1]
    halfway = columns // 2
    point_count = mem_hbm.shape[1]
    wall_count = wall_hbm.shape[1]
    own_points = force_hbm.shape[2]
    shard_width = lag_hbm.shape[2]
    block = 3 * wall_count

    loads = [
        pltpu.make_async_copy(given, held, load_sem.at[at])
        for at, (given, held) in enumerate(
            (
                (order_hbm, order_ref),
                (mem_hbm, mem_all.at[cell]),
                (wall_hbm, wall_all.at[wall, 0]),
                (normal_hbm, wall_all.at[wall, 1]),
                (lag_hbm, lag_all.at[cell, wall]),
                (data_hbm, data_all.at[wall]),
            )
        )
    ]

    partner = 2 * chip + other_core
    across = 2 * other_chip + core
    diagonal = 2 * other_chip + other_core
    peers = (partner, diagonal, across)

    barrier = pltpu.get_barrier_semaphore()
    for peer in peers:
        pl.semaphore_signal(barrier, inc=1, device_id={"wall": peer}, device_id_type=MESH)
    for target in range(cells - 1, 0, -1):

        @pl.when(target > cell)
        def _(target=target):
            for peer in (*peers, wall):
                pl.semaphore_signal(
                    barrier, inc=1, device_id={"cell": target, "wall": peer}, device_id_type=MESH
                )

    for load in loads:
        load.start()

    def force_copy(to_cell, to_chip, slot):
        return pltpu.make_async_remote_copy(
            force_hbm,
            force_all.at[cell, chip],
            force_send.at[slot, to_chip],
            force_recv.at[cell, chip],
            device_id={"cell": to_cell, "wall": 2 * to_chip + other_core},
            device_id_type=MESH,
        )

    def lag_copy(to_cell, to_wall, slot):
        return pltpu.make_async_remote_copy(
            lag_hbm,
            lag_all.at[cell, wall],
            lag_send.at[slot, to_wall],
            lag_recv.at[cell, wall],
            device_id={"cell": to_cell, "wall": to_wall},
            device_id_type=MESH,
        )

    def mem_copy(to_cell, slot):
        return pltpu.make_async_remote_copy(
            mem_hbm,
            mem_all.at[cell],
            mem_send.at[slot],
            mem_recv.at[cell],
            device_id={"cell": to_cell, "wall": partner},
            device_id_type=MESH,
        )

    def wall_copy(given, at, to_wall):
        return pltpu.make_async_remote_copy(
            given,
            wall_all.at[wall, at],
            wall_send.at[to_wall, at],
            wall_recv.at[wall, at],
            device_id={"wall": to_wall},
            device_id_type=MESH,
        )

    def data_copy(to_wall):
        return pltpu.make_async_remote_copy(
            data_hbm,
            data_all.at[wall],
            data_send.at[to_wall],
            data_recv.at[wall],
            device_id={"wall": to_wall},
            device_id_type=MESH,
        )

    def far_copies(target):
        copies = [mem_copy(target, target)]
        copies += [force_copy(target, to_chip, target) for to_chip in (other_chip, chip)]
        copies += [lag_copy(target, peer, target) for peer in (*peers, wall)]
        return copies

    def near_copies():
        copies = [wall_copy(wall_hbm, 0, peer) for peer in peers]
        copies += [wall_copy(normal_hbm, 1, peer) for peer in peers]
        copies += [force_copy(cell, to_chip, cells) for to_chip in (other_chip, chip)]
        copies += [data_copy(peer) for peer in peers]
        copies += [lag_copy(cell, peer, cells) for peer in peers]
        return copies

    pl.semaphore_wait(barrier, walls - 1 + walls * cell)

    for target in range(cells - 1):

        @pl.when(target < cell)
        def _(target=target):
            for copy in far_copies(target):
                copy.start()
            pl.semaphore_signal(
                ready.at[cell],
                inc=1,
                device_id={"cell": target, "wall": partner},
                device_id_type=MESH,
            )

    for copy in near_copies():
        copy.start()

    for load in loads[:4]:
        load.wait()

    order_row = order_ref[...]
    row_ids = lax.broadcasted_iota(jnp.int32, (columns, columns), 0)
    col_ids = lax.broadcasted_iota(jnp.int32, (columns, columns), 1)
    scatter = (row_ids == order_row).astype(jnp.float32).astype(jnp.bfloat16)
    unit = (row_ids == col_ids).astype(jnp.float32).astype(jnp.bfloat16)
    gather_f32 = lax.dot_general(unit, scatter, NT, preferred_element_type=jnp.float32)
    turned = ((row_ids == order_row) & (col_ids >= halfway)).astype(jnp.float32)
    is_first = jnp.sum(turned, axis=1, keepdims=True) > 0.5
    paired = jnp.concatenate([gather_f32[halfway:], gather_f32[:halfway]], axis=0)
    swap_f32 = jnp.dot(scatter, paired.astype(jnp.bfloat16), preferred_element_type=jnp.float32)
    swap = swap_f32.astype(jnp.bfloat16)

    def spread_wall(source):
        for j in range(3):
            wall_cols[source, j] = jnp.broadcast_to(
                wall_all[source, 0, j : j + 1, :], (LANES, wall_count)
            ).T

    for j in range(3):
        mem_cols[j] = jnp.broadcast_to(mem_all[cell, j : j + 1, :], (LANES, point_count)).T

    lane_ids = lax.broadcasted_iota(jnp.int32, (8, LANES), 1)

    def mem_rows(source):
        rows = []
        for j in range(3):
            low = jnp.broadcast_to(mem_all[source, j : j + 1, :LANES], (8, LANES))
            high = jnp.broadcast_to(mem_all[source, j : j + 1, LANES:], (8, LANES))
            low = pltpu.roll(low, own_points * other_core, 1)
            high = pltpu.roll(high, own_points * core, 1)
            rows.append(jnp.where(lane_ids < own_points, low, high)[0:1])
        return rows

    def fill_single(source, rows, at):
        apart = [wall_cols[at, j] - rows[j] for j in range(3)]
        square = apart[0] * apart[0] + apart[1] * apart[1] + apart[2] * apart[2]
        inverse = lax.rsqrt(square)
        scaled = stokes_coef * inverse
        cube = scaled * (inverse * inverse)
        for j in range(3):
            along = apart[j] * cube
            for i in range(j + 1):
                element = along * apart[i]
                if i == j:
                    element = element + scaled
                element = element.astype(jnp.bfloat16)
                for a, b in {(i, j), (j, i)}:
                    single_all[source, at, a, :, b * LANES : (b + 1) * LANES] = element

    def fill_double(source):
        own = pl.ds(pl.multiple_of(wall * own_points, own_points), own_points)
        apart = [mem_cols[j, own, :] - wall_all[source, 0, j : j + 1, :] for j in range(3)]
        square = apart[0] * apart[0] + apart[1] * apart[1] + apart[2] * apart[2]
        inverse = lax.rsqrt(square)
        flux = (
            apart[0] * wall_all[source, 1, 0:1, :]
            + apart[1] * wall_all[source, 1, 1:2, :]
            + apart[2] * wall_all[source, 1, 2:3, :]
        )
        inverse_square = inverse * inverse
        fifth = inverse_square * inverse_square * inverse
        weight = (-6.0 * stokes_coef) * flux * fifth
        for j in range(3):
            along = apart[j] * weight
            for i in range(j + 1):
                element = (along * apart[i]).astype(jnp.bfloat16)
                for a, b in {(i, j), (j, i)}:
                    double_all[
                        source,
                        a * own_points : (a + 1) * own_points,
                        b * wall_count : (b + 1) * wall_count,
                    ] = element

    own_rows = mem_rows(cell)
    spread_wall(wall)
    fill_single(cell, own_rows, wall)
    fill_double(wall)

    for peer in peers:
        for at in range(2):
            pltpu.make_async_remote_copy(
                wall_all.at[peer, at],
                wall_all.at[peer, at],
                wall_send.at[peer, at],
                wall_recv.at[peer, at],
                device_id={"wall": peer},
                device_id_type=MESH,
            ).wait_recv()
        spread_wall(peer)
        fill_single(cell, own_rows, peer)
        fill_double(peer)

    for target in range(1, cells):

        @pl.when(target > cell)
        def _(target=target):
            pl.semaphore_wait(ready.at[target], 1)
            for copy in far_copies(target):
                copy.start()

    def wait_force(source, at):
        pltpu.make_async_remote_copy(
            force_all.at[source, at],
            force_all.at[source, at],
            force_send.at[0, at],
            force_recv.at[source, at],
            device_id={"wall": partner},
            device_id_type=MESH,
        ).wait_recv()

    def single_layer(source):
        for at in range(2):
            wait_force(source, at)
        loaded = jnp.concatenate(
            [force_all[source, at, j] for j in range(3) for at in range(2)], axis=1
        )
        loaded = jnp.dot(swap, loaded, preferred_element_type=jnp.float32).astype(jnp.bfloat16)
        return lax.dot_general(
            loaded,
            single_all[source].reshape(walls * block, 3 * LANES),
            NT,
            preferred_element_type=jnp.float32,
        )

    partial = single_layer(cell)
    for load in loads[4:]:
        load.wait()
    for peer in peers:
        pltpu.make_async_remote_copy(
            data_all.at[peer],
            data_all.at[peer],
            data_send.at[peer],
            data_recv.at[peer],
            device_id={"wall": peer},
            device_id_type=MESH,
        ).wait_recv()
    for source in range(walls):
        for i in range(3):
            data_all[source, i] = jnp.dot(
                swap_f32, data_all[source, i], precision=lax.Precision.HIGHEST
            )

    for step in range(1, cells):
        source = jnp.where(cell + step < cells, cell + step, cells - 1 - step)
        pltpu.make_async_remote_copy(
            mem_all.at[source],
            mem_all.at[source],
            mem_send.at[0],
            mem_recv.at[source],
            device_id={"wall": partner},
            device_id_type=MESH,
        ).wait_recv()
        rows = mem_rows(source)
        for at in range(walls):
            fill_single(source, rows, at)
        partial = partial + single_layer(source)
    part_mine[...] = partial
    exchange = pltpu.make_async_remote_copy(
        part_mine,
        part_other,
        part_send,
        part_recv,
        device_id={"wall": partner},
        device_id_type=MESH,
    )
    exchange.start()

    def wait_lag(source, at):
        pltpu.make_async_remote_copy(
            lag_all.at[source, at],
            lag_all.at[source, at],
            lag_send.at[0, at],
            lag_recv.at[source, at],
            device_id={"wall": partner},
            device_id_type=MESH,
        ).wait_recv()

    for peer in peers:
        wait_lag(cell, peer)
    for step in range(1, cells):
        source = jnp.where(cell + step < cells, cell + step, cells - 1 - step)
        for at in range(walls):
            wait_lag(source, at)
    lag = jnp.concatenate(
        [lag_all[c, at, j] for at in range(walls) for j in range(3) for c in range(cells)], axis=1
    )
    placed_lag = jnp.dot(scatter[:, :halfway], lag, preferred_element_type=jnp.float32)

    for target in range(cells):

        @pl.when(target != cell)
        def _(target=target):
            for copy in far_copies(target):
                copy.wait_send()

    for copy in near_copies():
        copy.wait_send()

    exchange.wait_recv()
    total = jnp.zeros((columns, 3 * own_points), jnp.float32)
    for source in range(walls):
        pieces = []
        for i in range(3):
            lanes = slice(source * block + i * wall_count, source * block + (i + 1) * wall_count)
            dense = 2.0 * (data_all[source, i] - (partial[:, lanes] + part_other[:, lanes]))
            pieces.append(jnp.where(is_first, dense, placed_lag[:, lanes]).astype(jnp.bfloat16))
        total = total + lax.dot_general(
            jnp.concatenate(pieces, axis=1),
            double_all[source],
            NT,
            preferred_element_type=jnp.float32,
        )
    for i in range(3):
        out_ref[i] = total[:, i * own_points : (i + 1) * own_points]

    shift = lax.rem((cells - cell) * shard_width, wall_count)
    for i in range(3):
        lanes = pl.ds(pl.multiple_of(wall * block + i * wall_count, wall_count), wall_count)
        dense = 2.0 * (data_all[wall, i] - (part_mine[:, lanes] + part_other[:, lanes]))
        dense = jnp.dot(gather_f32[:halfway], dense, precision=lax.Precision.HIGHEST)
        density_ref[i] = pltpu.roll(dense, shift, 1)[:, :shard_width]
    exchange.wait_send()


def write_kernel(velocity_ref, density_ref, velocity_hbm, density_hbm, sem):
    first = pltpu.make_async_copy(velocity_ref, velocity_hbm, sem.at[0])
    second = pltpu.make_async_copy(density_ref, density_hbm, sem.at[1])
    first.start()
    second.start()
    first.wait()
    second.wait()


def fused_shards(cells, walls, mem_pos, forces, wall_pos, wall_normal, wall_data, lag_density, batch_order):
    columns = forces.shape[0]
    halfway = columns // 2
    point_count = mem_pos.shape[1]
    wall_count = wall_pos.shape[1]
    own_points = forces.shape[2]
    shard_width = lag_density.shape[2]
    dma = pltpu.SemaphoreType.DMA
    vmem = pl.BlockSpec(memory_space=pltpu.VMEM)
    hbm = pl.BlockSpec(memory_space=pltpu.HBM)
    velocity, density = pl.pallas_call(
        functools.partial(fused_kernel, cells, walls),
        out_shape=(
            pltpu.VMEM((3, columns, own_points), jnp.float32),
            pltpu.VMEM((3, halfway, shard_width), jnp.float32),
        ),
        in_specs=[hbm] * 7,
        out_specs=(vmem, vmem),
        scratch_shapes=[
            pltpu.VMEM((1, columns), jnp.int32),
            pltpu.VMEM((cells, 2, 3, columns, own_points), jnp.bfloat16),
            pltpu.VMEM((cells, walls, 3, halfway, shard_width), jnp.bfloat16),
            pltpu.VMEM((cells, 3, point_count), jnp.float32),
            pltpu.VMEM((walls, 2, 3, wall_count), jnp.float32),
            pltpu.VMEM((walls, 3, columns, wall_count), jnp.float32),
            pltpu.VMEM((walls, 3, wall_count, LANES), jnp.float32),
            pltpu.VMEM((3, point_count, LANES), jnp.float32),
            pltpu.VMEM((cells, walls, 3, wall_count, 3 * LANES), jnp.bfloat16),
            pltpu.VMEM((walls, 3 * own_points, 3 * wall_count), jnp.bfloat16),
            pltpu.VMEM((columns, walls * 3 * wall_count), jnp.float32),
            pltpu.VMEM((columns, walls * 3 * wall_count), jnp.float32),
            dma((6,)),
            dma((cells + 1, 2)),
            dma((cells, 2)),
            dma((cells + 1, walls)),
            dma((cells, walls)),
            dma((cells,)),
            dma((cells,)),
            dma((walls, 2)),
            dma((walls, 2)),
            dma((walls,)),
            dma((walls,)),
            dma,
            dma,
            pltpu.SemaphoreType.REGULAR((cells,)),
        ],
        compiler_params=pltpu.CompilerParams(
            collective_id=0, has_side_effects=True, vmem_limit_bytes=VMEM_GRANT
        ),
        name="coupling",
    )(
        mem_pos,
        jnp.transpose(forces, (1, 0, 2)),
        wall_pos,
        wall_normal,
        jnp.transpose(wall_data, (1, 0, 2)),
        jnp.transpose(lag_density, (1, 0, 2)),
        batch_order.reshape(1, columns),
    )
    velocity, density = pl.pallas_call(
        write_kernel,
        out_shape=(
            jax.ShapeDtypeStruct(velocity.shape, velocity.dtype),
            jax.ShapeDtypeStruct(density.shape, density.dtype),
        ),
        in_specs=[vmem] * 2,
        out_specs=(hbm, hbm),
        scratch_shapes=[dma((2,))],
        compiler_params=pltpu.CompilerParams(vmem_limit_bytes=1024 * 1024),
        name="write",
    )(velocity, density)
    return (jnp.transpose(velocity, (1, 0, 2)), jnp.transpose(density, (1, 0, 2)))


VMEM_GRANT = 60 * 1024 * 1024


def step(cells, walls, mem_pos, forces, wall_pos, *rest):
    point_count = mem_pos.shape[1]
    wall_count = wall_pos.shape[1]
    own_points = forces.shape[2]
    shard_width = rest[2].shape[2]
    tiles = 18 * walls * wall_count * (cells * LANES + own_points)
    fits = tiles <= VMEM_GRANT // 2
    aligned = (
        walls == 4
        and wall_count == LANES
        and 2 * own_points == LANES
        and point_count == walls * own_points
        and wall_count == cells * shard_width
    )
    if fits and aligned:
        return fused_shards(cells, walls, mem_pos, forces, wall_pos, *rest)
    return shards(mem_pos, forces, wall_pos, *rest)


def solution(mesh):
    placed = (
        P(None, ("groups", "cell")),
        P(None, None, ("groups", "cell", "wall")),
        P(None, ("groups", "wall")),
        P(None, ("groups", "wall")),
        P(None, None, ("groups", "wall")),
        P(None, None, ("groups", "wall", "cell")),
        P(),
    )
    return jax.shard_map(
        functools.partial(step, mesh.shape["cell"], mesh.shape["wall"]),
        mesh=mesh,
        in_specs=placed,
        out_specs=(
            P(None, None, ("groups", "cell", "wall")),
            P(None, None, ("groups", "wall", "cell")),
        ),
        check_vma=False,
    )
```

time: 16.8 us -> 19.8 us (1.18)
  the two profiles are of different devices: /device:TPU:0 before, /device:TPU:24 now
where the time goes in v1:
time: 19.8 us; the launch traced here: 19.7 us
  Pallas kernels  19 us (96%)
  between operations  0.64 us (3%)
    pallas_call x1, Pallas kernels, fused_shards(): pl.pallas_call(functools.partial(fused_kernel, cells, walls), out_shape=(...  18.4 us
    pallas_call x1, Pallas kernels, fused_shards(): pl.pallas_call(write_kernel, out_shape=(jax.ShapeDtypeStruct(velocity.sha...  0.64 us

profile of v1, /device:TPU:24, one launch (start us, length us, event | category | flops | bytes accessed | tf_op | source)
XLA Modules:
  0.0 19.7 jit_solution(2603693413410278740)
XLA Ops:
  0.6 18.4 %coupling.1 = (f32[3,32,64]{2,1,0:T(8,128)S(1)}, f32[3,16,32]{2,1,0:T(8,128)S(1)}) custom-call(f32[3,256]{1,0:T(4,128)} %mem_hbm.1, bf16[3,32,64]{2,1,0:T(8,128)(2,1)} %bitcast.7, f32[3,128]{1,0:T(4,128)} %wall_hbm.1, f32[3,128]{1,0:T(4,128)} %normal_hbm.1, f32[3,32,128]{2,1,0:T(8,128)} %bitcast.6, bf16[3,16,32]{2,1,0:T(8,128)(2,1)} %bitcast.8, s32[1,32]{1,0:T(1,128)} %bitcast.9), custom_call_target="tpu_custom_call" | custom-call | tf_op jit(solution)/shard_map/coupling/pallas_call | solution.py:533
  19.0 0.6 %write.1 = (f32[3,32,64]{2,1,0:T(8,128)}, f32[3,16,32]{2,1,0:T(8,128)}) custom-call(f32[3,32,64]{2,1,0:T(8,128)S(1)} %get-tuple-element.6.velocity_ref, f32[3,16,32]{2,1,0:T(8,128)S(1)} %get-tuple-element.7.density_ref), custom_call_target="tpu_custom_call" | custom-call | tf_op jit(solution)/shard_map/write/pallas_call | solution.py:582

commit v2 on v1

--- a/solution.py
+++ b/solution.py
@@ -128,8 +128,11 @@
     out_ref,
     density_ref,
     order_ref,
-    force_all,
-    lag_all,
+    force_ref,
+    lag_ref,
+    data_ref,
+    blocks,
+    passed,
     mem_all,
     wall_all,
     data_all,
@@ -139,11 +142,13 @@
     double_all,
     part_mine,
     part_other,
+    rest_mine,
+    rest_other,
     load_sem,
-    force_send,
-    force_recv,
-    lag_send,
-    lag_recv,
+    block_send,
+    block_recv,
+    pass_send,
+    pass_recv,
     mem_send,
     mem_recv,
     wall_send,
@@ -164,8 +169,8 @@
     halfway = columns // 2
     point_count = mem_hbm.shape[1]
     wall_count = wall_hbm.shape[1]
-    own_points = force_hbm.shape[2]
-    shard_width = lag_hbm.shape[2]
+    own_points = force_ref.shape[2]
+    shard_width = lag_ref.shape[2]
     block = 3 * wall_count
 
     loads = [
@@ -173,14 +178,17 @@
         for at, (given, held) in enumerate(
             (
                 (order_hbm, order_ref),
+                (force_hbm, force_ref),
+                (lag_hbm, lag_ref),
                 (mem_hbm, mem_all.at[cell]),
                 (wall_hbm, wall_all.at[wall, 0]),
                 (normal_hbm, wall_all.at[wall, 1]),
-                (lag_hbm, lag_all.at[cell, wall]),
-                (data_hbm, data_all.at[wall]),
+                (data_hbm, data_ref),
             )
         )
     ]
+    for load in loads:
+        load.start()
 
     partner = 2 * chip + other_core
     across = 2 * other_chip + core
@@ -194,31 +202,57 @@
 
         @pl.when(target > cell)
         def _(target=target):
-            for peer in (*peers, wall):
+            for to_chip in range(2):
                 pl.semaphore_signal(
-                    barrier, inc=1, device_id={"cell": target, "wall": peer}, device_id_type=MESH
+                    barrier,
+                    inc=1,
+                    device_id={"cell": target, "wall": 2 * to_chip + other_core},
+                    device_id_type=MESH,
                 )
 
-    for load in loads:
-        load.start()
-
-    def force_copy(to_cell, to_chip, slot):
+    loads[0].wait()
+    order_row = order_ref[...]
+    row_ids = lax.broadcasted_iota(jnp.int32, (columns, columns), 0)
+    col_ids = lax.broadcasted_iota(jnp.int32, (columns, columns), 1)
+    scatter = (row_ids == order_row).astype(jnp.float32).astype(jnp.bfloat16)
+    unit = (row_ids == col_ids).astype(jnp.float32).astype(jnp.bfloat16)
+    gather_f32 = lax.dot_general(unit, scatter, NT, preferred_element_type=jnp.float32)
+    gather = gather_f32.astype(jnp.bfloat16)
+
+    loads[1].wait()
+    rows = [jnp.dot(gather, force_ref[j], preferred_element_type=jnp.float32) for j in range(3)]
+    loads[2].wait()
+    lag_rows = [lag_ref[j].astype(jnp.float32) for j in range(3)]
+    spare = jnp.zeros((halfway, own_points - 2 * shard_width), jnp.float32)
+    unused = jnp.zeros((halfway, own_points - shard_width), jnp.float32)
+    halves = (
+        ([row[:halfway] for row in rows], (lag_rows[0], lag_rows[1], spare)),
+        ([row[halfway:] for row in rows], (lag_rows[2], unused)),
+    )
+    for wave, (part, rest) in enumerate(halves):
+        rest = [piece for piece in rest if piece.shape[1]]
+        pair = jnp.concatenate([part[0], part[1]], axis=1)
+        blocks[wave, core, cell, chip, 0] = pair.astype(jnp.bfloat16)
+        pair = jnp.concatenate([part[2], *rest], axis=1)
+        blocks[wave, core, cell, chip, 1] = pair.astype(jnp.bfloat16)
+
+    def block_copy(wave, to_cell, to_chip, slot):
         return pltpu.make_async_remote_copy(
-            force_hbm,
-            force_all.at[cell, chip],
-            force_send.at[slot, to_chip],
-            force_recv.at[cell, chip],
+            blocks.at[wave, core, cell, chip],
+            blocks.at[wave, core, cell, chip],
+            block_send.at[wave, slot, to_chip],
+            block_recv.at[wave, cell, chip],
             device_id={"cell": to_cell, "wall": 2 * to_chip + other_core},
             device_id_type=MESH,
         )
 
-    def lag_copy(to_cell, to_wall, slot):
+    def pass_copy(wave, source, at):
         return pltpu.make_async_remote_copy(
-            lag_hbm,
-            lag_all.at[cell, wall],
-            lag_send.at[slot, to_wall],
-            lag_recv.at[cell, wall],
-            device_id={"cell": to_cell, "wall": to_wall},
+            blocks.at[wave, other_core, source, at, 1],
+            passed.at[wave, source, at],
+            pass_send.at[wave, source, at],
+            pass_recv.at[wave, source, at],
+            device_id={"wall": partner},
             device_id_type=MESH,
         )
 
@@ -244,7 +278,7 @@
 
     def data_copy(to_wall):
         return pltpu.make_async_remote_copy(
-            data_hbm,
+            data_all.at[wall],
             data_all.at[wall],
             data_send.at[to_wall],
             data_recv.at[wall],
@@ -254,19 +288,18 @@
 
     def far_copies(target):
         copies = [mem_copy(target, target)]
-        copies += [force_copy(target, to_chip, target) for to_chip in (other_chip, chip)]
-        copies += [lag_copy(target, peer, target) for peer in (*peers, wall)]
+        for wave in range(2):
+            copies += [block_copy(wave, target, to, target) for to in (other_chip, chip)]
         return copies
 
     def near_copies():
         copies = [wall_copy(wall_hbm, 0, peer) for peer in peers]
         copies += [wall_copy(normal_hbm, 1, peer) for peer in peers]
-        copies += [force_copy(cell, to_chip, cells) for to_chip in (other_chip, chip)]
-        copies += [data_copy(peer) for peer in peers]
-        copies += [lag_copy(cell, peer, cells) for peer in peers]
+        for wave in range(2):
+            copies += [block_copy(wave, cell, to, cells) for to in (other_chip, chip)]
         return copies
 
-    pl.semaphore_wait(barrier, walls - 1 + walls * cell)
+    pl.semaphore_wait(barrier, walls - 1 + 2 * cell)
 
     for target in range(cells - 1):
 
@@ -284,20 +317,8 @@
     for copy in near_copies():
         copy.start()
 
-    for load in loads[:4]:
+    for load in loads[3:6]:
         load.wait()
-
-    order_row = order_ref[...]
-    row_ids = lax.broadcasted_iota(jnp.int32, (columns, columns), 0)
-    col_ids = lax.broadcasted_iota(jnp.int32, (columns, columns), 1)
-    scatter = (row_ids == order_row).astype(jnp.float32).astype(jnp.bfloat16)
-    unit = (row_ids == col_ids).astype(jnp.float32).astype(jnp.bfloat16)
-    gather_f32 = lax.dot_general(unit, scatter, NT, preferred_element_type=jnp.float32)
-    turned = ((row_ids == order_row) & (col_ids >= halfway)).astype(jnp.float32)
-    is_first = jnp.sum(turned, axis=1, keepdims=True) > 0.5
-    paired = jnp.concatenate([gather_f32[halfway:], gather_f32[:halfway]], axis=0)
-    swap_f32 = jnp.dot(scatter, paired.astype(jnp.bfloat16), preferred_element_type=jnp.float32)
-    swap = swap_f32.astype(jnp.bfloat16)
 
     def spread_wall(source):
         for j in range(3):
@@ -361,6 +382,14 @@
                     ] = element
 
     own_rows = mem_rows(cell)
+    loads[6].wait()
+    data_rows = [
+        jnp.dot(gather_f32, data_ref[j], precision=lax.Precision.HIGHEST) for j in range(3)
+    ]
+    for j in range(3):
+        data_all[wall, j] = data_rows[j][:halfway]
+    for peer in peers:
+        data_copy(peer).start()
     spread_wall(wall)
     fill_single(cell, own_rows, wall)
     fill_double(wall)
@@ -387,50 +416,41 @@
             for copy in far_copies(target):
                 copy.start()
 
-    def wait_force(source, at):
-        pltpu.make_async_remote_copy(
-            force_all.at[source, at],
-            force_all.at[source, at],
-            force_send.at[0, at],
-            force_recv.at[source, at],
-            device_id={"wall": partner},
-            device_id_type=MESH,
-        ).wait_recv()
-
-    def single_layer(source):
+    def loaded(wave, source):
         for at in range(2):
-            wait_force(source, at)
-        loaded = jnp.concatenate(
-            [force_all[source, at, j] for j in range(3) for at in range(2)], axis=1
-        )
-        loaded = jnp.dot(swap, loaded, preferred_element_type=jnp.float32).astype(jnp.bfloat16)
+            pltpu.make_async_remote_copy(
+                blocks.at[wave, other_core, source, at],
+                blocks.at[wave, other_core, source, at],
+                block_send.at[wave, 0, at],
+                block_recv.at[wave, source, at],
+                device_id={"wall": partner},
+                device_id_type=MESH,
+            ).wait_recv()
+        for at in range(2):
+            pass_copy(wave, source, at).start()
+        pairs = [blocks[wave, other_core, source, at, 0] for at in range(2)]
+        thirds = [blocks[wave, other_core, source, at, 1] for at in range(2)]
+        pieces = [piece[:, :own_points] for piece in pairs]
+        pieces += [piece[:, own_points:] for piece in pairs]
+        pieces += [piece[:, :own_points] for piece in thirds]
+        return jnp.concatenate(pieces, axis=1)
+
+    def first_layer(source):
         return lax.dot_general(
-            loaded,
+            loaded(0, source),
             single_all[source].reshape(walls * block, 3 * LANES),
             NT,
             preferred_element_type=jnp.float32,
         )
 
-    partial = single_layer(cell)
-    for load in loads[4:]:
-        load.wait()
-    for peer in peers:
-        pltpu.make_async_remote_copy(
-            data_all.at[peer],
-            data_all.at[peer],
-            data_send.at[peer],
-            data_recv.at[peer],
-            device_id={"wall": peer},
-            device_id_type=MESH,
-        ).wait_recv()
-    for source in range(walls):
-        for i in range(3):
-            data_all[source, i] = jnp.dot(
-                swap_f32, data_all[source, i], precision=lax.Precision.HIGHEST
-            )
-
+    def source_at(step):
+        if step == 0:
+            return cell
+        return jnp.where(cell + step < cells, cell + step, cells - 1 - step)
+
+    partial = first_layer(cell)
     for step in range(1, cells):
-        source = jnp.where(cell + step < cells, cell + step, cells - 1 - step)
+        source = source_at(step)
         pltpu.make_async_remote_copy(
             mem_all.at[source],
             mem_all.at[source],
@@ -442,38 +462,61 @@
         rows = mem_rows(source)
         for at in range(walls):
             fill_single(source, rows, at)
-        partial = partial + single_layer(source)
+        partial = partial + first_layer(source)
     part_mine[...] = partial
-    exchange = pltpu.make_async_remote_copy(
-        part_mine,
-        part_other,
-        part_send,
-        part_recv,
-        device_id={"wall": partner},
-        device_id_type=MESH,
-    )
-    exchange.start()
-
-    def wait_lag(source, at):
-        pltpu.make_async_remote_copy(
-            lag_all.at[source, at],
-            lag_all.at[source, at],
-            lag_send.at[0, at],
-            lag_recv.at[source, at],
+
+    def part_copy(given, held, at):
+        return pltpu.make_async_remote_copy(
+            given,
+            held,
+            part_send.at[at],
+            part_recv.at[at],
             device_id={"wall": partner},
             device_id_type=MESH,
-        ).wait_recv()
-
-    for peer in peers:
-        wait_lag(cell, peer)
-    for step in range(1, cells):
-        source = jnp.where(cell + step < cells, cell + step, cells - 1 - step)
-        for at in range(walls):
-            wait_lag(source, at)
-    lag = jnp.concatenate(
-        [lag_all[c, at, j] for at in range(walls) for j in range(3) for c in range(cells)], axis=1
-    )
-    placed_lag = jnp.dot(scatter[:, :halfway], lag, preferred_element_type=jnp.float32)
+        )
+
+    exchange = part_copy(part_mine, part_other, 0)
+    exchange.start()
+
+    rest = [jnp.zeros((halfway, block), jnp.float32) for _ in range(2)]
+    for step in range(cells):
+        source = source_at(step)
+        left = loaded(1, source)
+        for at, target in enumerate((wall, partner)):
+            rest[at] = rest[at] + lax.dot_general(
+                left,
+                single_all[source, target].reshape(block, 3 * LANES),
+                NT,
+                preferred_element_type=jnp.float32,
+            )
+    rest_mine[...] = rest[1]
+    rest_exchange = part_copy(rest_mine, rest_other, 1)
+    rest_exchange.start()
+
+    lag_places = ((0, own_points), (0, own_points + shard_width), (1, own_points))
+    for wave in range(2):
+        for source in range(cells):
+            for at in range(2):
+                pass_copy(wave, source, at).wait_recv()
+    lag_of = {}
+    for at in range(2):
+        for wave, start in lag_places:
+            for k in range(cells):
+                direct = blocks[wave, other_core, k, at, 1, :, start : start + shard_width]
+                handed = passed[wave, k, at, :, start : start + shard_width]
+                lag_of.setdefault((at, 0), []).append(direct)
+                lag_of.setdefault((at, 1), []).append(handed)
+    total = jnp.zeros((columns, 3 * own_points), jnp.float32)
+    for at in range(2):
+        for mine in range(2):
+            lag = jnp.concatenate(lag_of[at, mine], axis=1)
+            placed = jnp.dot(scatter[:, :halfway], lag, preferred_element_type=jnp.float32)
+            total = total + lax.dot_general(
+                placed.astype(jnp.bfloat16),
+                double_all[2 * at + (core if mine else other_core)],
+                NT,
+                preferred_element_type=jnp.float32,
+            )
 
     for target in range(cells):
 
@@ -484,31 +527,45 @@
 
     for copy in near_copies():
         copy.wait_send()
+    for peer in peers:
+        data_copy(peer).wait_send()
+        pltpu.make_async_remote_copy(
+            data_all.at[peer],
+            data_all.at[peer],
+            data_send.at[peer],
+            data_recv.at[peer],
+            device_id={"wall": peer},
+            device_id_type=MESH,
+        ).wait_recv()
+    for wave in range(2):
+        for source in range(cells):
+            for at in range(2):
+                pass_copy(wave, source, at).wait_send()
 
     exchange.wait_recv()
-    total = jnp.zeros((columns, 3 * own_points), jnp.float32)
     for source in range(walls):
         pieces = []
         for i in range(3):
             lanes = slice(source * block + i * wall_count, source * block + (i + 1) * wall_count)
             dense = 2.0 * (data_all[source, i] - (partial[:, lanes] + part_other[:, lanes]))
-            pieces.append(jnp.where(is_first, dense, placed_lag[:, lanes]).astype(jnp.bfloat16))
+            pieces.append(dense.astype(jnp.bfloat16))
+        placed = jnp.dot(
+            scatter[:, halfway:], jnp.concatenate(pieces, axis=1), preferred_element_type=jnp.float32
+        )
         total = total + lax.dot_general(
-            jnp.concatenate(pieces, axis=1),
-            double_all[source],
-            NT,
-            preferred_element_type=jnp.float32,
+            placed.astype(jnp.bfloat16), double_all[source], NT, preferred_element_type=jnp.float32
         )
     for i in range(3):
         out_ref[i] = total[:, i * own_points : (i + 1) * own_points]
 
+    rest_exchange.wait_recv()
     shift = lax.rem((cells - cell) * shard_width, wall_count)
     for i in range(3):
-        lanes = pl.ds(pl.multiple_of(wall * block + i * wall_count, wall_count), wall_count)
-        dense = 2.0 * (data_all[wall, i] - (part_mine[:, lanes] + part_other[:, lanes]))
-        dense = jnp.dot(gather_f32[:halfway], dense, precision=lax.Precision.HIGHEST)
+        lanes = slice(i * wall_count, (i + 1) * wall_count)
+        dense = 2.0 * (data_rows[i][halfway:] - (rest[0][:, lanes] + rest_other[:, lanes]))
         density_ref[i] = pltpu.roll(dense, shift, 1)[:, :shard_width]
     exchange.wait_send()
+    rest_exchange.wait_send()
 
 
 def write_kernel(velocity_ref, density_ref, velocity_hbm, density_hbm, sem):
@@ -540,30 +597,35 @@
         out_specs=(vmem, vmem),
         scratch_shapes=[
             pltpu.VMEM((1, columns), jnp.int32),
-            pltpu.VMEM((cells, 2, 3, columns, own_points), jnp.bfloat16),
-            pltpu.VMEM((cells, walls, 3, halfway, shard_width), jnp.bfloat16),
+            pltpu.VMEM((3, columns, own_points), jnp.bfloat16),
+            pltpu.VMEM((3, halfway, shard_width), jnp.bfloat16),
+            pltpu.VMEM((3, columns, wall_count), jnp.float32),
+            pltpu.VMEM((2, 2, cells, 2, 2, halfway, 2 * own_points), jnp.bfloat16),
+            pltpu.VMEM((2, cells, 2, halfway, 2 * own_points), jnp.bfloat16),
             pltpu.VMEM((cells, 3, point_count), jnp.float32),
             pltpu.VMEM((walls, 2, 3, wall_count), jnp.float32),
-            pltpu.VMEM((walls, 3, columns, wall_count), jnp.float32),
+            pltpu.VMEM((walls, 3, halfway, wall_count), jnp.float32),
             pltpu.VMEM((walls, 3, wall_count, LANES), jnp.float32),
             pltpu.VMEM((3, point_count, LANES), jnp.float32),
             pltpu.VMEM((cells, walls, 3, wall_count, 3 * LANES), jnp.bfloat16),
             pltpu.VMEM((walls, 3 * own_points, 3 * wall_count), jnp.bfloat16),
-            pltpu.VMEM((columns, walls * 3 * wall_count), jnp.float32),
-            pltpu.VMEM((columns, walls * 3 * wall_count), jnp.float32),
-            dma((6,)),
-            dma((cells + 1, 2)),
-            dma((cells, 2)),
-            dma((cells + 1, walls)),
-            dma((cells, walls)),
+            pltpu.VMEM((halfway, walls * 3 * wall_count), jnp.float32),
+            pltpu.VMEM((halfway, walls * 3 * wall_count), jnp.float32),
+            pltpu.VMEM((halfway, 3 * wall_count), jnp.float32),
+            pltpu.VMEM((halfway, 3 * wall_count), jnp.float32),
+            dma((7,)),
+            dma((2, cells + 1, 2)),
+            dma((2, cells, 2)),
+            dma((2, cells, 2)),
+            dma((2, cells, 2)),
             dma((cells,)),
             dma((cells,)),
             dma((walls, 2)),
             dma((walls, 2)),
             dma((walls,)),
             dma((walls,)),
-            dma,
-            dma,
+            dma((2,)),
+            dma((2,)),
             pltpu.SemaphoreType.REGULAR((cells,)),
         ],
         compiler_params=pltpu.CompilerParams(
@@ -610,6 +672,7 @@
         and 2 * own_points == LANES
         and point_count == walls * own_points
         and wall_count == cells * shard_width
+        and 2 * shard_width <= own_points
     )
     if fits and aligned:
         return fused_shards(cells, walls, mem_pos, forces, wall_pos, *rest)

time: 19.8 us -> 16.1 us (0.81)
  the two profiles are of different devices: /device:TPU:24 before, /device:TPU:28 now
where the time goes in v2:
time: 16.1 us; the launch traced here: 15.9 us
  Pallas kernels  15.3 us (95%)
  between operations  0.64 us (4%)
    pallas_call x1, Pallas kernels, fused_shards(): pl.pallas_call(functools.partial(fused_kernel, cells, walls), out_shape=(...  14.6 us
    pallas_call x1, Pallas kernels, fused_shards(): pl.pallas_call(write_kernel, out_shape=(jax.ShapeDtypeStruct(velocity.sha...  0.64 us

profile of v2, /device:TPU:28, one launch (start us, length us, event | category | flops | bytes accessed | tf_op | source)
XLA Modules:
  0.0 15.9 jit_solution(12255079834374368968)
XLA Ops:
  0.6 14.6 %coupling.1 = (f32[3,32,64]{2,1,0:T(8,128)S(1)}, f32[3,16,32]{2,1,0:T(8,128)S(1)}) custom-call(f32[3,256]{1,0:T(4,128)} %mem_hbm.1, bf16[3,32,64]{2,1,0:T(8,128)(2,1)} %bitcast.7, f32[3,128]{1,0:T(4,128)} %wall_hbm.1, f32[3,128]{1,0:T(4,128)} %normal_hbm.1, f32[3,32,128]{2,1,0:T(8,128)} %bitcast.6, bf16[3,16,32]{2,1,0:T(8,128)(2,1)} %bitcast.8, s32[1,32]{1,0:T(1,128)} %bitcast.9), custom_call_target="tpu_custom_call" | custom-call | tf_op jit(solution)/shard_map/coupling/pallas_call | solution.py:590
  15.2 0.6 %write.1 = (f32[3,32,64]{2,1,0:T(8,128)}, f32[3,16,32]{2,1,0:T(8,128)}) custom-call(f32[3,32,64]{2,1,0:T(8,128)S(1)} %get-tuple-element.6.velocity_ref, f32[3,16,32]{2,1,0:T(8,128)S(1)} %get-tuple-element.7.density_ref), custom_call_target="tpu_custom_call" | custom-call | tf_op jit(solution)/shard_map/write/pallas_call | solution.py:644

commit v3 on v1

v3 whole, which is shorter than its diff:
```python
import functools
import math

import jax
import jax.numpy as jnp
from jax import lax
from jax.experimental import pallas as pl
from jax.experimental.pallas import tpu as pltpu
from jax.sharding import PartitionSpec as P

stokes_coef = 1.0 / (8.0 * math.pi)


def single_tile(targets, sources):
    separation = targets[:, None, :] - sources[:, :, None]
    inverse = lax.rsqrt(jnp.sum(separation * separation, axis=0))
    inverse_cube = inverse * inverse * inverse
    stacked = []
    for second_dim in range(3):
        entries_row = []
        for first_dim in range(3):
            element = separation[first_dim] * separation[second_dim] * inverse_cube
            if first_dim == second_dim:
                element = element + inverse
            entries_row.append(element * stokes_coef)
        stacked.append(jnp.stack(entries_row, axis=1))
    kernel_tile = jnp.stack(stacked, axis=0)
    return kernel_tile.reshape(3 * sources.shape[1], 3 * targets.shape[1]).astype(jnp.bfloat16)


def double_tile(targets, sources, normals):
    separation = targets[:, None, :] - sources[:, :, None]
    inverse = lax.rsqrt(jnp.sum(separation * separation, axis=0))
    normal_flux = jnp.sum(separation * normals[:, :, None], axis=0)
    weight = -6.0 * stokes_coef * normal_flux * inverse**5
    stacked = []
    for second_dim in range(3):
        entries_row = []
        for first_dim in range(3):
            entries_row.append(weight * separation[first_dim] * separation[second_dim])
        stacked.append(jnp.stack(entries_row, axis=1))
    kernel_tile = jnp.stack(stacked, axis=0)
    return kernel_tile.reshape(3 * sources.shape[1], 3 * targets.shape[1]).astype(jnp.bfloat16)


def shards(mem_pos, forces, wall_pos, wall_normal, wall_data, lag_density, batch_order):
    columns = forces.shape[0]
    halfway = columns // 2
    point_count = mem_pos.shape[1]
    wall_count = wall_pos.shape[1]
    shard_width = lag_density.shape[2]
    piece_len = math.gcd(point_count, 128)
    block_count = point_count // piece_len
    first_rows = batch_order[:halfway]
    second_rows = batch_order[halfway:]
    force_block = lax.all_gather(forces, "wall", axis=2, tiled=True)
    lag_block = lax.all_gather(lag_density, "cell", axis=2, tiled=True)
    lag_flat = lag_block.reshape(halfway, 3 * wall_count)

    def position_at(block_index):
        return lax.dynamic_slice_in_dim(mem_pos, block_index * piece_len, piece_len, 1)

    def single_term(block_index):
        loaded = lax.dynamic_slice_in_dim(force_block, block_index * piece_len, piece_len, 2)
        loaded = loaded.reshape(columns, 3 * piece_len)
        return jnp.dot(
            loaded,
            single_tile(wall_pos, position_at(block_index)),
            preferred_element_type=jnp.float32,
        )

    def double_term(dense_rows, block_index):
        kernel_tile = double_tile(position_at(block_index), wall_pos, wall_normal)
        product = jnp.dot(dense_rows, kernel_tile, preferred_element_type=jnp.float32)
        return product.reshape(dense_rows.shape[0], 3, piece_len)

    def place_block(target, piece, block_index):
        return lax.dynamic_update_slice_in_dim(target, piece, block_index * piece_len, 2)

    empty_wall = jnp.zeros((columns, 3 * wall_count), jnp.float32)

    def add_single(block_index, running):
        return running + single_term(block_index)

    running = lax.fori_loop(0, block_count, add_single, empty_wall)
    wall_term = running.reshape(columns, 3, wall_count)
    position_cell = lax.axis_index("cell")
    first_sum = lax.psum(jnp.take(wall_term, first_rows, axis=0), "cell")
    first_block = (2.0 * (jnp.take(wall_data, first_rows, axis=0) - first_sum)).astype(jnp.bfloat16)
    second_sum = lax.psum_scatter(
        jnp.take(wall_term, second_rows, axis=0).astype(jnp.bfloat16),
        "cell",
        scatter_dimension=2,
        tiled=True,
    ).astype(jnp.float32)
    second_data = lax.dynamic_slice_in_dim(
        jnp.take(wall_data, second_rows, axis=0), position_cell * shard_width, shard_width, 2
    )
    wall_density = 2.0 * (second_data - second_sum)
    first_flat = first_block.reshape(halfway, 3 * wall_count)
    carried = jnp.concatenate([lag_flat, first_flat], axis=0)

    def all_terms(block_index, target):
        return place_block(target, double_term(carried, block_index), block_index)

    membrane_term = lax.fori_loop(
        0, block_count, all_terms, jnp.zeros((columns, 3, point_count), jnp.float32)
    )
    batched = lax.psum_scatter(membrane_term, "wall", scatter_dimension=2, tiled=True)
    membrane_velocity = jnp.zeros_like(batched).at[batch_order].set(batched)
    return (membrane_velocity, wall_density)

LANES = 128
MESH = pl.DeviceIdType.MESH
NT = (((1,), (1,)), ((), ()))


def fused_kernel(
    cells,
    walls,
    mem_hbm,
    force_hbm,
    wall_hbm,
    normal_hbm,
    data_hbm,
    lag_hbm,
    order_hbm,
    out_ref,
    density_ref,
    order_ref,
    order_smem,
    force_ref,
    lag_ref,
    data_ref,
    own_block,
    own_lag,
    block_all,
    second_all,
    lag_all,
    lag_pass,
    mem_all,
    wall_all,
    data_all,
    wall_cols,
    mem_cols,
    single_all,
    single_rest,
    double_all,
    part_mine,
    part_other,
    share_out,
    share_in,
    load_sem,
    block_send,
    block_recv,
    second_send,
    second_recv,
    lag_send,
    lag_recv,
    pass_send,
    pass_recv,
    mem_send,
    mem_recv,
    wall_send,
    wall_recv,
    data_send,
    data_recv,
    part_send,
    part_recv,
    share_send,
    share_recv,
    ready,
    ready_near,
):
    cell = lax.axis_index("cell")
    wall = lax.axis_index("wall")
    chip = lax.div(wall, 2)
    core = lax.rem(wall, 2)
    other_core = 1 - core
    other_chip = 1 - chip
    columns = order_ref.shape[1]
    halfway = columns // 2
    point_count = mem_hbm.shape[1]
    wall_count = wall_hbm.shape[1]
    own_points = force_ref.shape[2]
    shard_width = lag_ref.shape[2]
    block = 3 * wall_count
    partner = 2 * chip + other_core

    loads = [
        pltpu.make_async_copy(given, held, load_sem.at[at])
        for at, (given, held) in enumerate(
            (
                (order_hbm, order_smem),
                (order_hbm, order_ref),
                (force_hbm, force_ref),
                (lag_hbm, lag_ref),
                (mem_hbm, mem_all.at[cell]),
                (wall_hbm, wall_all.at[wall, 0]),
                (normal_hbm, wall_all.at[wall, 1]),
                (data_hbm, data_ref),
            )
        )
    ]
    for load in loads:
        load.start()

    barrier = pltpu.get_barrier_semaphore()
    for to_cell in range(cells - 1, -1, -1):
        for to_wall in range(walls):

            @pl.when((to_cell > cell) | ((to_cell == cell) & (to_wall > wall)))
            def _(to_cell=to_cell, to_wall=to_wall):
                pl.semaphore_signal(
                    barrier,
                    inc=1,
                    device_id={"cell": to_cell, "wall": to_wall},
                    device_id_type=MESH,
                )

    below = walls * cell + wall

    @pl.when(below > 0)
    def _():
        pl.semaphore_wait(barrier, below)

    for to_cell in range(cells - 1):
        for to_wall in range(walls):

            @pl.when(to_cell < cell)
            def _(to_cell=to_cell, to_wall=to_wall):
                pl.semaphore_signal(
                    ready.at[cell],
                    inc=1,
                    device_id={"cell": to_cell, "wall": to_wall},
                    device_id_type=MESH,
                )

    for to_wall in range(walls - 1):

        @pl.when(to_wall < wall)
        def _(to_wall=to_wall):
            pl.semaphore_signal(
                ready_near.at[wall], inc=1, device_id={"wall": to_wall}, device_id_type=MESH
            )

    def remote(given, held, send, recv, **to):
        return pltpu.make_async_remote_copy(
            given, held, send, recv, device_id=to, device_id_type=MESH
        )

    def block_copy(to_cell, to_chip):
        return remote(
            own_block,
            block_all.at[cell, chip],
            block_send,
            block_recv.at[cell],
            cell=to_cell,
            wall=2 * to_chip + other_core,
        )

    def lag_copy(to_cell, to_chip):
        return remote(
            own_lag,
            lag_all.at[cell, chip],
            lag_send,
            lag_recv,
            cell=to_cell,
            wall=2 * to_chip + other_core,
        )

    def mem_copy(to_cell):
        return remote(
            mem_hbm,
            mem_all.at[cell],
            mem_send,
            mem_recv.at[cell],
            cell=to_cell,
            wall=partner,
        )

    def share_copy(to_cell):
        return remote(
            share_out.at[to_cell],
            share_in.at[cell],
            share_send,
            share_recv,
            cell=to_cell,
        )

    def wall_copies(to_wall):
        return [
            remote(
                given,
                wall_all.at[wall, at],
                wall_send,
                wall_recv.at[wall],
                wall=to_wall,
            )
            for at, given in enumerate((wall_hbm, normal_hbm))
        ]

    def second_copy(to_wall):
        held = second_all.at[wall]
        return remote(
            held, held, second_send, second_recv, wall=to_wall
        )

    def data_copy(to_wall):
        held = data_all.at[wall]
        return remote(held, held, data_send, data_recv, wall=to_wall)

    def near_walls(body):
        for to_wall in range(walls):

            @pl.when(to_wall != wall)
            def _(to_wall=to_wall):
                body(to_wall)

    def far_cells(test, body):
        for to_cell in range(cells):

            @pl.when(test(to_cell))
            def _(to_cell=to_cell):
                body(to_cell)

    def start_blocks(to_cell):
        for to_chip in (other_chip, chip):
            block_copy(to_cell, to_chip).start()

    def start_lag(to_cell):
        for to_chip in (other_chip, chip):
            lag_copy(to_cell, to_chip).start()

    for to_wall in range(walls):

        @pl.when(to_wall < wall)
        def _(to_wall=to_wall):
            for copy in wall_copies(to_wall):
                copy.start()

    far_cells(lambda to_cell: to_cell < cell, lambda to_cell: mem_copy(to_cell).start())

    row_ids = lax.broadcasted_iota(jnp.int32, (columns, columns), 0)
    col_ids = lax.broadcasted_iota(jnp.int32, (columns, columns), 1)
    loads[0].wait()
    wanted = jnp.zeros((columns, columns), jnp.int32)
    for k in range(columns):
        wanted = jnp.where(row_ids == k, order_smem[0, k], wanted)
    gather_f32 = (wanted == col_ids).astype(jnp.float32)
    gather = gather_f32.astype(jnp.bfloat16)

    loads[2].wait()
    rows = [jnp.dot(gather, force_ref[j], preferred_element_type=jnp.float32) for j in range(3)]
    folded = halfway // 2
    part = [row[:halfway] for row in rows]
    pair = jnp.concatenate([part[0], part[1]], axis=1)
    last = jnp.concatenate([part[2][:folded], part[2][folded:]], axis=1)
    own_block[...] = jnp.concatenate([pair, last], axis=0).astype(jnp.bfloat16)

    far_cells(lambda to_cell: to_cell < cell, start_blocks)

    part = [row[halfway:] for row in rows]
    unused = jnp.zeros((halfway, LANES - own_points), jnp.float32)
    second_all[wall, 0] = jnp.concatenate([part[0], part[1]], axis=1).astype(jnp.bfloat16)
    second_all[wall, 1] = jnp.concatenate([part[2], unused], axis=1).astype(jnp.bfloat16)

    loads[3].wait()
    pieces = [lag_ref[j].astype(jnp.float32) for j in range(3)]
    if LANES > 3 * shard_width:
        pieces.append(jnp.zeros((halfway, LANES - 3 * shard_width), jnp.float32))
    own_lag[...] = jnp.concatenate(pieces, axis=1).astype(jnp.bfloat16)

    far_cells(lambda to_cell: to_cell < cell, start_lag)

    def start_near(to_wall):
        @pl.when(to_wall > wall)
        def _():
            pl.semaphore_wait(ready_near.at[to_wall], 1)
            for copy in wall_copies(to_wall):
                copy.start()

        @pl.when(to_wall % 2 != core)
        def _():
            block_copy(cell, to_wall // 2).start()

        second_copy(to_wall).start()

        @pl.when(to_wall % 2 != core)
        def _():
            lag_copy(cell, to_wall // 2).start()


    near_walls(start_near)

    for load in loads[4:]:
        load.wait()
    data_rows = [
        jnp.dot(gather_f32, data_ref[j], precision=lax.Precision.HIGHEST) for j in range(3)
    ]
    for j in range(3):
        data_all[wall, j] = data_rows[j][:halfway]
    near_walls(lambda to_wall: data_copy(to_wall).start())

    loads[1].wait()
    scatter = (row_ids == order_ref[...]).astype(jnp.float32).astype(jnp.bfloat16)

    def spread_wall(source):
        for j in range(3):
            wall_cols[source, j] = jnp.broadcast_to(
                wall_all[source, 0, j : j + 1, :], (LANES, wall_count)
            ).T

    for j in range(3):
        mem_cols[j] = jnp.broadcast_to(mem_all[cell, j : j + 1, :], (LANES, point_count)).T

    lane_ids = lax.broadcasted_iota(jnp.int32, (8, LANES), 1)

    def mem_rows(source, parity):
        rows = []
        for j in range(3):
            low = jnp.broadcast_to(mem_all[source, j : j + 1, :LANES], (8, LANES))
            high = jnp.broadcast_to(mem_all[source, j : j + 1, LANES:], (8, LANES))
            low = pltpu.roll(low, own_points * parity, 1)
            high = pltpu.roll(high, own_points * (1 - parity), 1)
            rows.append(jnp.where(lane_ids < own_points, low, high)[0:1])
        return rows

    def fill_single(tile, rows, at):
        apart = [wall_cols[at, j] - rows[j] for j in range(3)]
        square = apart[0] * apart[0] + apart[1] * apart[1] + apart[2] * apart[2]
        inverse = lax.rsqrt(square)
        scaled = stokes_coef * inverse
        cube = scaled * (inverse * inverse)
        for j in range(3):
            along = apart[j] * cube
            for i in range(j + 1):
                element = along * apart[i]
                if i == j:
                    element = element + scaled
                element = element.astype(jnp.bfloat16)
                for a, b in {(i, j), (j, i)}:
                    tile[a, :, b * LANES : (b + 1) * LANES] = element

    def fill_double(source):
        own = pl.ds(pl.multiple_of(wall * own_points, own_points), own_points)
        apart = [mem_cols[j, own, :] - wall_all[source, 0, j : j + 1, :] for j in range(3)]
        square = apart[0] * apart[0] + apart[1] * apart[1] + apart[2] * apart[2]
        inverse = lax.rsqrt(square)
        flux = (
            apart[0] * wall_all[source, 1, 0:1, :]
            + apart[1] * wall_all[source, 1, 1:2, :]
            + apart[2] * wall_all[source, 1, 2:3, :]
        )
        inverse_square = inverse * inverse
        fifth = inverse_square * inverse_square * inverse
        weight = (-6.0 * stokes_coef) * flux * fifth
        for j in range(3):
            along = apart[j] * weight
            for i in range(j + 1):
                element = (along * apart[i]).astype(jnp.bfloat16)
                for a, b in {(i, j), (j, i)}:
                    lanes = pl.multiple_of(source * block + b * wall_count, wall_count)
                    double_all[
                        a * own_points : (a + 1) * own_points, pl.ds(lanes, wall_count)
                    ] = element

    own_rows = mem_rows(cell, other_core)
    spread_wall(wall)
    fill_single(single_all.at[cell, wall], own_rows, wall)
    fill_single(single_rest, mem_rows(cell, core), wall)
    fill_double(wall)

    def wait_into(held, recv):
        remote(held, held, load_sem.at[0], recv, wall=partner).wait_recv()

    def wait_out(held, send):
        remote(held, held, send, load_sem.at[0], wall=partner).wait_send()

    peers = (partner, 2 * other_chip + other_core, 2 * other_chip + core)

    def take_wall(peer):
        wait_into(wall_all.at[peer], wall_recv.at[peer])
        spread_wall(peer)
        fill_single(single_all.at[cell, peer], own_rows, peer)
        fill_double(peer)

    def start_above(up):
        def body(to_cell):
            pl.semaphore_wait(ready.at[to_cell], walls)
            mem_copy(to_cell).start()
            start_blocks(to_cell)
            start_lag(to_cell)

        far_cells(lambda to_cell: to_cell == cell + up, body)

    def second_columns(tiles):
        pieces = [tile[0][:, :own_points] for tile in tiles]
        pieces += [tile[0][:, own_points:] for tile in tiles]
        pieces += [tile[1][:, :own_points] for tile in tiles]
        return jnp.concatenate(pieces, axis=1)

    def columns_of(tiles):
        tiles = [tile.astype(jnp.float32) for tile in tiles]
        pieces = [tile[:halfway, :own_points] for tile in tiles]
        pieces += [tile[:halfway, own_points:] for tile in tiles]
        for tile in tiles:
            last = tile[halfway:]
            pieces.append(jnp.concatenate([last[:, :own_points], last[:, own_points:]], axis=0))
        return jnp.concatenate(pieces, axis=1).astype(jnp.bfloat16)

    take_wall(partner)
    start_above(1)
    take_wall(peers[1])
    for up in range(2, cells - 1):
        start_above(up)

    wait_into(second_all.at[: walls - 1], second_recv)
    share = jnp.zeros((halfway, block), jnp.float32)
    for parity, tile in ((other_core, single_all.at[cell, wall]), (core, single_rest)):
        share = share + lax.dot_general(
            second_columns([second_all[2 * at + parity] for at in range(2)]),
            tile[...].reshape(block, 3 * LANES),
            NT,
            preferred_element_type=jnp.float32,
        )
    own_share = jnp.zeros((halfway, LANES), jnp.float32)
    for to_cell in range(cells):
        pieces = [
            share[:, i * wall_count + to_cell * shard_width :][:, :shard_width] for i in range(3)
        ]
        if LANES > 3 * shard_width:
            pieces.append(jnp.zeros((halfway, LANES - 3 * shard_width), jnp.float32))
        piece = jnp.concatenate(pieces, axis=1)
        own_share = jnp.where(cell == to_cell, piece, own_share)
        share_out[to_cell] = piece.astype(jnp.bfloat16)
    far_cells(lambda to_cell: to_cell < cell, lambda to_cell: share_copy(to_cell).start())
    if cells > 2:
        start_above(cells - 1)
    far_cells(lambda to_cell: to_cell > cell, lambda to_cell: share_copy(to_cell).start())
    take_wall(peers[2])

    def source_at(step):
        if step == 0:
            return cell
        return jnp.where(cell + step < cells, cell + step, cells - 1 - step)

    def take_mem(step):
        source = source_at(step)
        wait_into(mem_all.at[source], mem_recv.at[source])
        rows = mem_rows(source, other_core)
        for at in range(walls):
            fill_single(single_all.at[source, at], rows, at)

    def first_layer(step):
        source = source_at(step)
        wait_into(block_all.at[source], block_recv.at[source])
        left = columns_of([block_all[source, at] for at in range(2)])
        return lax.dot_general(
            left,
            single_all[source].reshape(walls * block, 3 * LANES),
            NT,
            preferred_element_type=jnp.float32,
        )

    partial = jnp.zeros((halfway, walls * block), jnp.float32)
    for step in range(cells):
        if step + 1 < cells:
            take_mem(step + 1)
        partial = partial + first_layer(step)
    part_mine[...] = partial
    exchange = remote(part_mine, part_other, part_send, part_recv, wall=partner)
    exchange.start()

    wait_into(lag_all, lag_recv)
    handing = remote(lag_all, lag_pass, pass_send, pass_recv, wall=partner)
    handing.start()

    wait_out(mem_all.at[: cells - 1], mem_send)
    wait_out(block_all, block_send)
    wait_out(lag_all, lag_send)
    wait_out(wall_all.at[: walls - 1], wall_send)
    wait_out(second_all.at[: walls - 1], second_send)
    wait_into(data_all.at[: walls - 1], data_recv)
    wait_out(data_all.at[: walls - 1], data_send)
    wait_out(share_in.at[: cells - 1], share_send)

    def layer(rows):
        return lax.dot_general(rows, double_all[...], NT, preferred_element_type=jnp.float32)

    handing.wait_recv()
    lag_row = []
    for at in range(2):
        for parity in range(2):
            lag_row += [
                jnp.where(core == parity, lag_pass[k, at], lag_all[k, at])[
                    :, j * shard_width : (j + 1) * shard_width
                ]
                for j in range(3)
                for k in range(cells)
            ]
    lag_part = layer(jnp.concatenate(lag_row, axis=1))

    exchange.wait_recv()
    pieces = []
    for source in range(walls):
        for i in range(3):
            lanes = slice(source * block + i * wall_count, source * block + (i + 1) * wall_count)
            dense = 2.0 * (data_all[source, i] - (part_mine[:, lanes] + part_other[:, lanes]))
            pieces.append(dense.astype(jnp.bfloat16))
    batched = jnp.concatenate([lag_part, layer(jnp.concatenate(pieces, axis=1))], axis=0)
    total = jnp.zeros((columns, 3 * own_points), jnp.float32)
    for _ in range(3):
        piece = batched.astype(jnp.bfloat16)
        total = total + jnp.dot(scatter, piece, preferred_element_type=jnp.float32)
        batched = batched - piece.astype(jnp.float32)
    for i in range(3):
        out_ref[i] = total[:, i * own_points : (i + 1) * own_points]

    wait_into(share_in.at[: cells - 1], share_recv)
    second_sum = own_share
    for step in range(1, cells):
        second_sum = second_sum + share_in[source_at(step)].astype(jnp.float32)
    shift = lax.rem((cells - cell) * shard_width, wall_count)
    for i in range(3):
        held = pltpu.roll(data_rows[i][halfway:], shift, 1)[:, :shard_width]
        density_ref[i] = 2.0 * (held - second_sum[:, i * shard_width : (i + 1) * shard_width])

    exchange.wait_send()
    handing.wait_send()


def write_kernel(velocity_ref, density_ref, velocity_hbm, density_hbm, sem):
    first = pltpu.make_async_copy(velocity_ref, velocity_hbm, sem.at[0])
    second = pltpu.make_async_copy(density_ref, density_hbm, sem.at[1])
    first.start()
    second.start()
    first.wait()
    second.wait()


def fused_shards(cells, walls, mem_pos, forces, wall_pos, wall_normal, wall_data, lag_density, batch_order):
    columns = forces.shape[0]
    halfway = columns // 2
    point_count = mem_pos.shape[1]
    wall_count = wall_pos.shape[1]
    own_points = forces.shape[2]
    shard_width = lag_density.shape[2]
    dma = pltpu.SemaphoreType.DMA
    vmem = pl.BlockSpec(memory_space=pltpu.VMEM)
    hbm = pl.BlockSpec(memory_space=pltpu.HBM)
    velocity, density = pl.pallas_call(
        functools.partial(fused_kernel, cells, walls),
        out_shape=(
            pltpu.VMEM((3, columns, own_points), jnp.float32),
            pltpu.VMEM((3, halfway, shard_width), jnp.float32),
        ),
        in_specs=[hbm] * 7,
        out_specs=(vmem, vmem),
        scratch_shapes=[
            pltpu.VMEM((1, columns), jnp.int32),
            pltpu.SMEM((1, columns), jnp.int32),
            pltpu.VMEM((3, columns, own_points), jnp.bfloat16),
            pltpu.VMEM((3, halfway, shard_width), jnp.bfloat16),
            pltpu.VMEM((3, columns, wall_count), jnp.float32),
            pltpu.VMEM((3 * halfway // 2, LANES), jnp.bfloat16),
            pltpu.VMEM((halfway, LANES), jnp.bfloat16),
            pltpu.VMEM((cells, 2, 3 * halfway // 2, LANES), jnp.bfloat16),
            pltpu.VMEM((walls, 2, halfway, LANES), jnp.bfloat16),
            pltpu.VMEM((cells, 2, halfway, LANES), jnp.bfloat16),
            pltpu.VMEM((cells, 2, halfway, LANES), jnp.bfloat16),
            pltpu.VMEM((cells, 3, point_count), jnp.float32),
            pltpu.VMEM((walls, 2, 3, wall_count), jnp.float32),
            pltpu.VMEM((walls, 3, halfway, wall_count), jnp.float32),
            pltpu.VMEM((walls, 3, wall_count, LANES), jnp.float32),
            pltpu.VMEM((3, point_count, LANES), jnp.float32),
            pltpu.VMEM((cells, walls, 3, wall_count, 3 * LANES), jnp.bfloat16),
            pltpu.VMEM((3, wall_count, 3 * LANES), jnp.bfloat16),
            pltpu.VMEM((3 * own_points, walls * 3 * wall_count), jnp.bfloat16),
            pltpu.VMEM((halfway, walls * 3 * wall_count), jnp.float32),
            pltpu.VMEM((halfway, walls * 3 * wall_count), jnp.float32),
            pltpu.VMEM((cells, halfway, LANES), jnp.bfloat16),
            pltpu.VMEM((cells, halfway, LANES), jnp.bfloat16),
            dma((8,)),
            dma,
            dma((cells,)),
            dma,
            dma,
            dma,
            dma,
            dma,
            dma,
            dma,
            dma((cells,)),
            dma,
            dma((walls,)),
            dma,
            dma,
            dma,
            dma,
            dma,
            dma,
            pltpu.SemaphoreType.REGULAR((cells,)),
            pltpu.SemaphoreType.REGULAR((walls,)),
        ],
        compiler_params=pltpu.CompilerParams(
            collective_id=0, has_side_effects=True, vmem_limit_bytes=VMEM_GRANT
        ),
        name="coupling",
    )(
        mem_pos,
        jnp.transpose(forces, (1, 0, 2)),
        wall_pos,
        wall_normal,
        jnp.transpose(wall_data, (1, 0, 2)),
        jnp.transpose(lag_density, (1, 0, 2)),
        batch_order.reshape(1, columns),
    )
    velocity, density = pl.pallas_call(
        write_kernel,
        out_shape=(
            jax.ShapeDtypeStruct(velocity.shape, velocity.dtype),
            jax.ShapeDtypeStruct(density.shape, density.dtype),
        ),
        in_specs=[vmem] * 2,
        out_specs=(hbm, hbm),
        scratch_shapes=[dma((2,))],
        compiler_params=pltpu.CompilerParams(vmem_limit_bytes=1024 * 1024),
        name="write",
    )(velocity, density)
    return (jnp.transpose(velocity, (1, 0, 2)), jnp.transpose(density, (1, 0, 2)))


VMEM_GRANT = 60 * 1024 * 1024


def step(cells, walls, mem_pos, forces, wall_pos, *rest):
    point_count = mem_pos.shape[1]
    wall_count = wall_pos.shape[1]
    own_points = forces.shape[2]
    shard_width = rest[2].shape[2]
    tiles = 18 * walls * wall_count * (cells * LANES + own_points)
    fits = tiles <= VMEM_GRANT // 2
    aligned = (
        walls == 4
        and wall_count == LANES
        and 2 * own_points == LANES
        and point_count == walls * own_points
        and wall_count == cells * shard_width
        and 3 * shard_width <= LANES
    )
    if fits and aligned:
        return fused_shards(cells, walls, mem_pos, forces, wall_pos, *rest)
    return shards(mem_pos, forces, wall_pos, *rest)


def solution(mesh):
    placed = (
        P(None, ("groups", "cell")),
        P(None, None, ("groups", "cell", "wall")),
        P(None, ("groups", "wall")),
        P(None, ("groups", "wall")),
        P(None, None, ("groups", "wall")),
        P(None, None, ("groups", "wall", "cell")),
        P(),
    )
    return jax.shard_map(
        functools.partial(step, mesh.shape["cell"], mesh.shape["wall"]),
        mesh=mesh,
        in_specs=placed,
        out_specs=(
            P(None, None, ("groups", "cell", "wall")),
            P(None, None, ("groups", "wall", "cell")),
        ),
        check_vma=False,
    )
```

time: 19.8 us -> 14.2 us (0.72)
  the two profiles are of different devices: /device:TPU:24 before, /device:TPU:27 now
where the time goes in v3:
time: 14.2 us; the launch traced here: 14 us
  Pallas kernels  13.4 us (94%)
  between operations  0.64 us (5%)
    pallas_call x1, Pallas kernels, fused_shards(): pl.pallas_call(functools.partial(fused_kernel, cells, walls), out_shape=(...  12.7 us
    pallas_call x1, Pallas kernels, fused_shards(): pl.pallas_call(write_kernel, out_shape=(jax.ShapeDtypeStruct(velocity.sha...  0.64 us

profile of v3, /device:TPU:27, one launch (start us, length us, event | category | flops | bytes accessed | tf_op | source)
XLA Modules:
  0.0 14.0 jit_solution(13328500416905717137)
XLA Ops:
  0.6 12.7 %coupling.1 = (f32[3,32,64]{2,1,0:T(8,128)S(1)}, f32[3,16,32]{2,1,0:T(8,128)S(1)}) custom-call(f32[3,256]{1,0:T(4,128)} %mem_hbm.1, bf16[3,32,64]{2,1,0:T(8,128)(2,1)} %bitcast.7, f32[3,128]{1,0:T(4,128)} %wall_hbm.1, f32[3,128]{1,0:T(4,128)} %normal_hbm.1, f32[3,32,128]{2,1,0:T(8,128)} %bitcast.6, bf16[3,16,32]{2,1,0:T(8,128)(2,1)} %bitcast.8, s32[1,32]{1,0:T(1,128)} %bitcast.9), custom_call_target="tpu_custom_call" | custom-call | tf_op jit(solution)/shard_map/coupling/pallas_call | solution.py:652
  13.4 0.6 %write.1 = (f32[3,32,64]{2,1,0:T(8,128)}, f32[3,16,32]{2,1,0:T(8,128)}) custom-call(f32[3,32,64]{2,1,0:T(8,128)S(1)} %get-tuple-element.6.velocity_ref, f32[3,16,32]{2,1,0:T(8,128)S(1)} %get-tuple-element.7.density_ref), custom_call_target="tpu_custom_call" | custom-call | tf_op jit(solution)/shard_map/write/pallas_call | solution.py:719

commit v4 on v3

--- a/solution.py
+++ b/solution.py
@@ -137,7 +137,6 @@
     block_all,
     second_all,
     lag_all,
-    lag_pass,
     mem_all,
     wall_all,
     data_all,
@@ -157,8 +156,6 @@
     second_recv,
     lag_send,
     lag_recv,
-    pass_send,
-    pass_recv,
     mem_send,
     mem_recv,
     wall_send,
@@ -259,14 +256,9 @@
             wall=2 * to_chip + other_core,
         )
 
-    def lag_copy(to_cell, to_chip):
+    def lag_copy(to_cell, to_wall):
         return remote(
-            own_lag,
-            lag_all.at[cell, chip],
-            lag_send,
-            lag_recv,
-            cell=to_cell,
-            wall=2 * to_chip + other_core,
+            own_lag, lag_all.at[cell * walls + wall], lag_send, lag_recv, cell=to_cell, wall=to_wall
         )
 
     def mem_copy(to_cell):
@@ -329,8 +321,8 @@
             block_copy(to_cell, to_chip).start()
 
     def start_lag(to_cell):
-        for to_chip in (other_chip, chip):
-            lag_copy(to_cell, to_chip).start()
+        for to_wall in range(walls):
+            lag_copy(to_cell, to_wall).start()
 
     for to_wall in range(walls):
 
@@ -358,18 +350,26 @@
     last = jnp.concatenate([part[2][:folded], part[2][folded:]], axis=1)
     own_block[...] = jnp.concatenate([pair, last], axis=0).astype(jnp.bfloat16)
 
-    far_cells(lambda to_cell: to_cell < cell, start_blocks)
-
     part = [row[halfway:] for row in rows]
     unused = jnp.zeros((halfway, LANES - own_points), jnp.float32)
     second_all[wall, 0] = jnp.concatenate([part[0], part[1]], axis=1).astype(jnp.bfloat16)
     second_all[wall, 1] = jnp.concatenate([part[2], unused], axis=1).astype(jnp.bfloat16)
 
+    for to_wall in range(walls - 1):
+
+        @pl.when(to_wall < wall)
+        def _(to_wall=to_wall):
+            second_copy(to_wall).start()
+
+    far_cells(lambda to_cell: to_cell < cell, start_blocks)
+
     loads[3].wait()
     pieces = [lag_ref[j].astype(jnp.float32) for j in range(3)]
     if LANES > 3 * shard_width:
         pieces.append(jnp.zeros((halfway, LANES - 3 * shard_width), jnp.float32))
-    own_lag[...] = jnp.concatenate(pieces, axis=1).astype(jnp.bfloat16)
+    packed_lag = jnp.concatenate(pieces, axis=1).astype(jnp.bfloat16)
+    own_lag[...] = packed_lag
+    lag_all[cell * walls + wall] = packed_lag
 
     far_cells(lambda to_cell: to_cell < cell, start_lag)
 
@@ -379,16 +379,13 @@
             pl.semaphore_wait(ready_near.at[to_wall], 1)
             for copy in wall_copies(to_wall):
                 copy.start()
+            second_copy(to_wall).start()
 
         @pl.when(to_wall % 2 != core)
         def _():
             block_copy(cell, to_wall // 2).start()
 
-        second_copy(to_wall).start()
-
-        @pl.when(to_wall % 2 != core)
-        def _():
-            lag_copy(cell, to_wall // 2).start()
+        lag_copy(cell, to_wall).start()
 
 
     near_walls(start_near)
@@ -490,7 +487,6 @@
             pl.semaphore_wait(ready.at[to_cell], walls)
             mem_copy(to_cell).start()
             start_blocks(to_cell)
-            start_lag(to_cell)
 
         far_cells(lambda to_cell: to_cell == cell + up, body)
 
@@ -538,6 +534,7 @@
     if cells > 2:
         start_above(cells - 1)
     far_cells(lambda to_cell: to_cell > cell, lambda to_cell: share_copy(to_cell).start())
+    far_cells(lambda to_cell: to_cell > cell, start_lag)
     take_wall(peers[2])
 
     def source_at(step):
@@ -552,61 +549,70 @@
         for at in range(walls):
             fill_single(single_all.at[source, at], rows, at)
 
-    def first_layer(step):
+    def first_columns(step):
         source = source_at(step)
         wait_into(block_all.at[source], block_recv.at[source])
-        left = columns_of([block_all[source, at] for at in range(2)])
-        return lax.dot_general(
-            left,
-            single_all[source].reshape(walls * block, 3 * LANES),
-            NT,
-            preferred_element_type=jnp.float32,
-        )
-
-    partial = jnp.zeros((halfway, walls * block), jnp.float32)
+        return columns_of([block_all[source, at] for at in range(2)])
+
+    def exchange(half):
+        return remote(
+            part_mine.at[half],
+            part_other.at[half],
+            part_send.at[half],
+            part_recv.at[half],
+            wall=partner,
+        )
+
+    width = walls // 2 * block
+    partial = [jnp.zeros((halfway, width), jnp.float32) for _ in range(2)]
     for step in range(cells):
         if step + 1 < cells:
             take_mem(step + 1)
-        partial = partial + first_layer(step)
-    part_mine[...] = partial
-    exchange = remote(part_mine, part_other, part_send, part_recv, wall=partner)
-    exchange.start()
-
-    wait_into(lag_all, lag_recv)
-    handing = remote(lag_all, lag_pass, pass_send, pass_recv, wall=partner)
-    handing.start()
+        left = first_columns(step)
+        for half in range(2):
+            tile = single_all[source_at(step), half * (walls // 2) : (half + 1) * (walls // 2)]
+            partial[half] = partial[half] + lax.dot_general(
+                left,
+                tile.reshape(width, 3 * LANES),
+                NT,
+                preferred_element_type=jnp.float32,
+            )
+            if step == cells - 1:
+                part_mine[half] = partial[half]
+                exchange(half).start()
 
     wait_out(mem_all.at[: cells - 1], mem_send)
     wait_out(block_all, block_send)
-    wait_out(lag_all, lag_send)
+    wait_out(lag_all.at[: cells * walls - 1], lag_send)
     wait_out(wall_all.at[: walls - 1], wall_send)
     wait_out(second_all.at[: walls - 1], second_send)
     wait_into(data_all.at[: walls - 1], data_recv)
     wait_out(data_all.at[: walls - 1], data_send)
     wait_out(share_in.at[: cells - 1], share_send)
 
+    wait_into(lag_all.at[: cells * walls - 1], lag_recv)
+
     def layer(rows):
         return lax.dot_general(rows, double_all[...], NT, preferred_element_type=jnp.float32)
 
-    handing.wait_recv()
     lag_row = []
-    for at in range(2):
-        for parity in range(2):
-            lag_row += [
-                jnp.where(core == parity, lag_pass[k, at], lag_all[k, at])[
-                    :, j * shard_width : (j + 1) * shard_width
-                ]
-                for j in range(3)
-                for k in range(cells)
-            ]
+    for source in range(walls):
+        lag_row += [
+            lag_all[k * walls + source, :, j * shard_width : (j + 1) * shard_width]
+            for j in range(3)
+            for k in range(cells)
+        ]
     lag_part = layer(jnp.concatenate(lag_row, axis=1))
 
-    exchange.wait_recv()
+    for half in range(2):
+        exchange(half).wait_recv()
     pieces = []
     for source in range(walls):
         for i in range(3):
-            lanes = slice(source * block + i * wall_count, source * block + (i + 1) * wall_count)
-            dense = 2.0 * (data_all[source, i] - (part_mine[:, lanes] + part_other[:, lanes]))
+            half, at = divmod(source, walls // 2)
+            lanes = slice(at * block + i * wall_count, at * block + (i + 1) * wall_count)
+            velocity = part_mine[half, :, lanes] + part_other[half, :, lanes]
+            dense = 2.0 * (data_all[source, i] - velocity)
             pieces.append(dense.astype(jnp.bfloat16))
     batched = jnp.concatenate([lag_part, layer(jnp.concatenate(pieces, axis=1))], axis=0)
     total = jnp.zeros((columns, 3 * own_points), jnp.float32)
@@ -626,8 +632,8 @@
         held = pltpu.roll(data_rows[i][halfway:], shift, 1)[:, :shard_width]
         density_ref[i] = 2.0 * (held - second_sum[:, i * shard_width : (i + 1) * shard_width])
 
-    exchange.wait_send()
-    handing.wait_send()
+    for half in range(2):
+        exchange(half).wait_send()
 
 
 def write_kernel(velocity_ref, density_ref, velocity_hbm, density_hbm, sem):
@@ -667,8 +673,7 @@
             pltpu.VMEM((halfway, LANES), jnp.bfloat16),
             pltpu.VMEM((cells, 2, 3 * halfway // 2, LANES), jnp.bfloat16),
             pltpu.VMEM((walls, 2, halfway, LANES), jnp.bfloat16),
-            pltpu.VMEM((cells, 2, halfway, LANES), jnp.bfloat16),
-            pltpu.VMEM((cells, 2, halfway, LANES), jnp.bfloat16),
+            pltpu.VMEM((cells * walls, halfway, LANES), jnp.bfloat16),
             pltpu.VMEM((cells, 3, point_count), jnp.float32),
             pltpu.VMEM((walls, 2, 3, wall_count), jnp.float32),
             pltpu.VMEM((walls, 3, halfway, wall_count), jnp.float32),
@@ -677,8 +682,8 @@
             pltpu.VMEM((cells, walls, 3, wall_count, 3 * LANES), jnp.bfloat16),
             pltpu.VMEM((3, wall_count, 3 * LANES), jnp.bfloat16),
             pltpu.VMEM((3 * own_points, walls * 3 * wall_count), jnp.bfloat16),
-            pltpu.VMEM((halfway, walls * 3 * wall_count), jnp.float32),
-            pltpu.VMEM((halfway, walls * 3 * wall_count), jnp.float32),
+            pltpu.VMEM((2, halfway, walls // 2 * 3 * wall_count), jnp.float32),
+            pltpu.VMEM((2, halfway, walls // 2 * 3 * wall_count), jnp.float32),
             pltpu.VMEM((cells, halfway, LANES), jnp.bfloat16),
             pltpu.VMEM((cells, halfway, LANES), jnp.bfloat16),
             dma((8,)),
@@ -689,15 +694,13 @@
             dma,
             dma,
             dma,
-            dma,
-            dma,
             dma((cells,)),
             dma,
             dma((walls,)),
             dma,
             dma,
-            dma,
-            dma,
+            dma((2,)),
+            dma((2,)),
             dma,
             dma,
             pltpu.SemaphoreType.REGULAR((cells,)),

time: 14.2 us -> 13.4 us (0.944)
  the two profiles are of different devices: /device:TPU:27 before, /device:TPU:0 now
where the time goes in v4:
time: 13.4 us; the launch traced here: 13.2 us
  Pallas kernels  12.6 us (94%)
  between operations  0.64 us (5%)
    pallas_call x1, Pallas kernels, fused_shards(): pl.pallas_call(functools.partial(fused_kernel, cells, walls), out_shape=(...  12 us
    pallas_call x1, Pallas kernels, fused_shards(): pl.pallas_call(write_kernel, out_shape=(jax.ShapeDtypeStruct(velocity.sha...  0.64 us

profile of v4, /device:TPU:0, one launch (start us, length us, event | category | flops | bytes accessed | tf_op | source)
XLA Modules:
  0.0 13.2 jit_solution(14611638463211820091)
XLA Ops:
  0.6 12.0 %coupling.1 = (f32[3,32,64]{2,1,0:T(8,128)S(1)}, f32[3,16,32]{2,1,0:T(8,128)S(1)}) custom-call(f32[3,256]{1,0:T(4,128)} %mem_hbm.1, bf16[3,32,64]{2,1,0:T(8,128)(2,1)} %bitcast.7, f32[3,128]{1,0:T(4,128)} %wall_hbm.1, f32[3,128]{1,0:T(4,128)} %normal_hbm.1, f32[3,32,128]{2,1,0:T(8,128)} %bitcast.6, bf16[3,16,32]{2,1,0:T(8,128)(2,1)} %bitcast.8, s32[1,32]{1,0:T(1,128)} %bitcast.9), custom_call_target="tpu_custom_call" | custom-call | tf_op jit(solution)/shard_map/coupling/pallas_call | solution.py:658
  12.6 0.6 %write.1 = (f32[3,32,64]{2,1,0:T(8,128)}, f32[3,16,32]{2,1,0:T(8,128)}) custom-call(f32[3,32,64]{2,1,0:T(8,128)S(1)} %get-tuple-element.6.velocity_ref, f32[3,16,32]{2,1,0:T(8,128)S(1)} %get-tuple-element.7.density_ref), custom_call_target="tpu_custom_call" | custom-call | tf_op jit(solution)/shard_map/write/pallas_call | solution.py:722

commit v5 on v4

--- a/solution.py
+++ b/solution.py
@@ -113,6 +113,9 @@
 LANES = 128
 MESH = pl.DeviceIdType.MESH
 NT = (((1,), (1,)), ((), ()))
+
+
+TILES = ((0, 0), (1, 1), (2, 2), (0, 1), (0, 2), (1, 2))
 
 
 def fused_kernel(
@@ -435,9 +438,8 @@
                 element = along * apart[i]
                 if i == j:
                     element = element + scaled
-                element = element.astype(jnp.bfloat16)
-                for a, b in {(i, j), (j, i)}:
-                    tile[a, :, b * LANES : (b + 1) * LANES] = element
+                at_tile = TILES.index((i, j))
+                tile[:, at_tile * LANES : (at_tile + 1) * LANES] = element.astype(jnp.bfloat16)
 
     def fill_double(source):
         own = pl.ds(pl.multiple_of(wall * own_points, own_points), own_points)
@@ -464,7 +466,7 @@
 
     own_rows = mem_rows(cell, other_core)
     spread_wall(wall)
-    fill_single(single_all.at[cell, wall], own_rows, wall)
+    fill_single(single_all.at[0, wall], own_rows, wall)
     fill_single(single_rest, mem_rows(cell, core), wall)
     fill_double(wall)
 
@@ -479,7 +481,7 @@
     def take_wall(peer):
         wait_into(wall_all.at[peer], wall_recv.at[peer])
         spread_wall(peer)
-        fill_single(single_all.at[cell, peer], own_rows, peer)
+        fill_single(single_all.at[0, peer], own_rows, peer)
         fill_double(peer)
 
     def start_above(up):
@@ -490,20 +492,38 @@
 
         far_cells(lambda to_cell: to_cell == cell + up, body)
 
+    low_lanes = lax.broadcasted_iota(jnp.int32, (halfway, LANES), 1) < own_points
+
+    def low_halves(first, second):
+        mask = low_lanes[: first.shape[0]]
+        return jnp.where(mask, first, pltpu.roll(second, own_points, 1))
+
+    def high_halves(first, second):
+        mask = low_lanes[: first.shape[0]]
+        return jnp.where(mask, pltpu.roll(first, own_points, 1), second)
+
+    def stack_rows(parts):
+        empty = jnp.zeros((halfway, LANES), jnp.bfloat16)
+        groups = []
+        for i in range(3):
+            row = [empty] * len(TILES)
+            for at_tile, (a, b) in enumerate(TILES):
+                if i in (a, b):
+                    row[at_tile] = parts[a + b - i].astype(jnp.bfloat16)
+            groups.append(jnp.concatenate(row, axis=1))
+        return jnp.concatenate(groups, axis=0)
+
     def second_columns(tiles):
-        pieces = [tile[0][:, :own_points] for tile in tiles]
-        pieces += [tile[0][:, own_points:] for tile in tiles]
-        pieces += [tile[1][:, :own_points] for tile in tiles]
-        return jnp.concatenate(pieces, axis=1)
+        pair = [tile[0].astype(jnp.float32) for tile in tiles]
+        last = [tile[1].astype(jnp.float32) for tile in tiles]
+        return stack_rows([low_halves(*pair), high_halves(*pair), low_halves(*last)])
 
     def columns_of(tiles):
         tiles = [tile.astype(jnp.float32) for tile in tiles]
-        pieces = [tile[:halfway, :own_points] for tile in tiles]
-        pieces += [tile[:halfway, own_points:] for tile in tiles]
-        for tile in tiles:
-            last = tile[halfway:]
-            pieces.append(jnp.concatenate([last[:, :own_points], last[:, own_points:]], axis=0))
-        return jnp.concatenate(pieces, axis=1).astype(jnp.bfloat16)
+        pair = [tile[:halfway] for tile in tiles]
+        last = [tile[halfway:] for tile in tiles]
+        last = jnp.concatenate([low_halves(*last), high_halves(*last)], axis=0)
+        return stack_rows([low_halves(*pair), high_halves(*pair), last])
 
     take_wall(partner)
     start_above(1)
@@ -512,18 +532,22 @@
         start_above(up)
 
     wait_into(second_all.at[: walls - 1], second_recv)
-    share = jnp.zeros((halfway, block), jnp.float32)
-    for parity, tile in ((other_core, single_all.at[cell, wall]), (core, single_rest)):
+    share = jnp.zeros((3 * halfway, wall_count), jnp.float32)
+    for parity, tile in ((other_core, single_all.at[0, wall]), (core, single_rest)):
         share = share + lax.dot_general(
             second_columns([second_all[2 * at + parity] for at in range(2)]),
-            tile[...].reshape(block, 3 * LANES),
+            tile[...],
             NT,
             preferred_element_type=jnp.float32,
         )
     own_share = jnp.zeros((halfway, LANES), jnp.float32)
     for to_cell in range(cells):
         pieces = [
-            share[:, i * wall_count + to_cell * shard_width :][:, :shard_width] for i in range(3)
+            share[
+                i * halfway : (i + 1) * halfway,
+                to_cell * shard_width : (to_cell + 1) * shard_width,
+            ]
+            for i in range(3)
         ]
         if LANES > 3 * shard_width:
             pieces.append(jnp.zeros((halfway, LANES - 3 * shard_width), jnp.float32))
@@ -542,12 +566,14 @@
             return cell
         return jnp.where(cell + step < cells, cell + step, cells - 1 - step)
 
-    def take_mem(step):
+    def wait_mem(step):
         source = source_at(step)
         wait_into(mem_all.at[source], mem_recv.at[source])
-        rows = mem_rows(source, other_core)
+
+    def take_mem(step):
+        rows = mem_rows(source_at(step), other_core)
         for at in range(walls):
-            fill_single(single_all.at[source, at], rows, at)
+            fill_single(single_all.at[step, at], rows, at)
 
     def first_columns(step):
         source = source_at(step)
@@ -563,23 +589,25 @@
             wall=partner,
         )
 
-    width = walls // 2 * block
-    partial = [jnp.zeros((halfway, width), jnp.float32) for _ in range(2)]
+    width = walls // 2 * wall_count
+    partial = [jnp.zeros((3 * halfway, width), jnp.float32) for _ in range(2)]
     for step in range(cells):
         if step + 1 < cells:
-            take_mem(step + 1)
+            wait_mem(step + 1)
         left = first_columns(step)
         for half in range(2):
-            tile = single_all[source_at(step), half * (walls // 2) : (half + 1) * (walls // 2)]
+            tile = single_all[step, half * (walls // 2) : (half + 1) * (walls // 2)]
             partial[half] = partial[half] + lax.dot_general(
                 left,
-                tile.reshape(width, 3 * LANES),
+                tile.reshape(width, len(TILES) * LANES),
                 NT,
                 preferred_element_type=jnp.float32,
             )
             if step == cells - 1:
                 part_mine[half] = partial[half]
                 exchange(half).start()
+        if step + 1 < cells:
+            take_mem(step + 1)
 
     wait_out(mem_all.at[: cells - 1], mem_send)
     wait_out(block_all, block_send)
@@ -610,8 +638,9 @@
     for source in range(walls):
         for i in range(3):
             half, at = divmod(source, walls // 2)
-            lanes = slice(at * block + i * wall_count, at * block + (i + 1) * wall_count)
-            velocity = part_mine[half, :, lanes] + part_other[half, :, lanes]
+            held = slice(i * halfway, (i + 1) * halfway)
+            lanes = slice(at * wall_count, (at + 1) * wall_count)
+            velocity = part_mine[half, held, lanes] + part_other[half, held, lanes]
             dense = 2.0 * (data_all[source, i] - velocity)
             pieces.append(dense.astype(jnp.bfloat16))
     batched = jnp.concatenate([lag_part, layer(jnp.concatenate(pieces, axis=1))], axis=0)
@@ -679,11 +708,11 @@
             pltpu.VMEM((walls, 3, halfway, wall_count), jnp.float32),
             pltpu.VMEM((walls, 3, wall_count, LANES), jnp.float32),
             pltpu.VMEM((3, point_count, LANES), jnp.float32),
-            pltpu.VMEM((cells, walls, 3, wall_count, 3 * LANES), jnp.bfloat16),
-            pltpu.VMEM((3, wall_count, 3 * LANES), jnp.bfloat16),
+            pltpu.VMEM((cells, walls, wall_count, len(TILES) * LANES), jnp.bfloat16),
+            pltpu.VMEM((wall_count, len(TILES) * LANES), jnp.bfloat16),
             pltpu.VMEM((3 * own_points, walls * 3 * wall_count), jnp.bfloat16),
-            pltpu.VMEM((2, halfway, walls // 2 * 3 * wall_count), jnp.float32),
-            pltpu.VMEM((2, halfway, walls // 2 * 3 * wall_count), jnp.float32),
+            pltpu.VMEM((2, 3 * halfway, walls // 2 * wall_count), jnp.float32),
+            pltpu.VMEM((2, 3 * halfway, walls // 2 * wall_count), jnp.float32),
             pltpu.VMEM((cells, halfway, LANES), jnp.bfloat16),
             pltpu.VMEM((cells, halfway, LANES), jnp.bfloat16),
             dma((8,)),

time: 13.4 us -> 13.2 us (0.985)
  Pallas kernels: 12.6 us -> 12.4 us
    pallas_call x1, Pallas kernels: 12 us -> 11.7 us  [fused_shards(): pl.pallas_call(functools.partial(fused_kernel, cells, walls), out_shape=(...]
where the time goes in v5:
time: 13.2 us; the launch traced here: 13 us
  Pallas kernels  12.4 us (94%)
  between operations  0.64 us (5%)
    pallas_call x1, Pallas kernels, fused_shards(): pl.pallas_call(functools.partial(fused_kernel, cells, walls), out_shape=(...  11.7 us
    pallas_call x1, Pallas kernels, fused_shards(): pl.pallas_call(write_kernel, out_shape=(jax.ShapeDtypeStruct(velocity.sha...  0.64 us

profile of v5, /device:TPU:0, one launch (start us, length us, event | category | flops | bytes accessed | tf_op | source)
XLA Modules:
  0.0 13.0 jit_solution(17618395195831943387)
XLA Ops:
  0.6 11.7 %coupling.1 = (f32[3,32,64]{2,1,0:T(8,128)S(1)}, f32[3,16,32]{2,1,0:T(8,128)S(1)}) custom-call(f32[3,256]{1,0:T(4,128)} %mem_hbm.1, bf16[3,32,64]{2,1,0:T(8,128)(2,1)} %bitcast.7, f32[3,128]{1,0:T(4,128)} %wall_hbm.1, f32[3,128]{1,0:T(4,128)} %normal_hbm.1, f32[3,32,128]{2,1,0:T(8,128)} %bitcast.6, bf16[3,16,32]{2,1,0:T(8,128)(2,1)} %bitcast.8, s32[1,32]{1,0:T(1,128)} %bitcast.9), custom_call_target="tpu_custom_call" | custom-call | tf_op jit(solution)/shard_map/coupling/pallas_call | solution.py:687
  12.4 0.6 %write.1 = (f32[3,32,64]{2,1,0:T(8,128)}, f32[3,16,32]{2,1,0:T(8,128)}) custom-call(f32[3,32,64]{2,1,0:T(8,128)S(1)} %get-tuple-element.6.velocity_ref, f32[3,16,32]{2,1,0:T(8,128)S(1)} %get-tuple-element.7.density_ref), custom_call_target="tpu_custom_call" | custom-call | tf_op jit(solution)/shard_map/write/pallas_call | solution.py:751

commit v6 on v5

--- a/solution.py
+++ b/solution.py
@@ -266,7 +266,7 @@
 
     def mem_copy(to_cell):
         return remote(
-            mem_hbm,
+            mem_all.at[cell],
             mem_all.at[cell],
             mem_send,
             mem_recv.at[cell],
@@ -281,19 +281,12 @@
             share_send,
             share_recv,
             cell=to_cell,
-        )
-
-    def wall_copies(to_wall):
-        return [
-            remote(
-                given,
-                wall_all.at[wall, at],
-                wall_send,
-                wall_recv.at[wall],
-                wall=to_wall,
-            )
-            for at, given in enumerate((wall_hbm, normal_hbm))
-        ]
+            wall=partner,
+        )
+
+    def wall_copy(to_wall):
+        held = wall_all.at[wall]
+        return remote(held, held, wall_send, wall_recv.at[wall], wall=to_wall)
 
     def second_copy(to_wall):
         held = second_all.at[wall]
@@ -327,14 +320,15 @@
         for to_wall in range(walls):
             lag_copy(to_cell, to_wall).start()
 
-    for to_wall in range(walls):
+    loads[4].wait()
+    far_cells(lambda to_cell: to_cell < cell, lambda to_cell: mem_copy(to_cell).start())
+    for load in loads[5:7]:
+        load.wait()
+    for to_wall in range(walls - 1):
 
         @pl.when(to_wall < wall)
         def _(to_wall=to_wall):
-            for copy in wall_copies(to_wall):
-                copy.start()
-
-    far_cells(lambda to_cell: to_cell < cell, lambda to_cell: mem_copy(to_cell).start())
+            wall_copy(to_wall).start()
 
     row_ids = lax.broadcasted_iota(jnp.int32, (columns, columns), 0)
     col_ids = lax.broadcasted_iota(jnp.int32, (columns, columns), 1)
@@ -376,25 +370,29 @@
 
     far_cells(lambda to_cell: to_cell < cell, start_lag)
 
+    for to_wall in range(1, walls):
+
+        @pl.when(to_wall > wall)
+        def _(to_wall=to_wall):
+            pl.semaphore_wait(ready_near.at[to_wall], 1)
+            wall_copy(to_wall).start()
+
     def start_near(to_wall):
         @pl.when(to_wall > wall)
         def _():
-            pl.semaphore_wait(ready_near.at[to_wall], 1)
-            for copy in wall_copies(to_wall):
-                copy.start()
             second_copy(to_wall).start()
 
         @pl.when(to_wall % 2 != core)
         def _():
             block_copy(cell, to_wall // 2).start()
 
+    def start_near_lag(to_wall):
         lag_copy(cell, to_wall).start()
 
-
     near_walls(start_near)
-
-    for load in loads[4:]:
-        load.wait()
+    near_walls(start_near_lag)
+
+    loads[7].wait()
     data_rows = [
         jnp.dot(gather_f32, data_ref[j], precision=lax.Precision.HIGHEST) for j in range(3)
     ]
@@ -467,7 +465,6 @@
     own_rows = mem_rows(cell, other_core)
     spread_wall(wall)
     fill_single(single_all.at[0, wall], own_rows, wall)
-    fill_single(single_rest, mem_rows(cell, core), wall)
     fill_double(wall)
 
     def wait_into(held, recv):
@@ -526,6 +523,7 @@
         return stack_rows([low_halves(*pair), high_halves(*pair), last])
 
     take_wall(partner)
+    fill_single(single_rest, mem_rows(cell, core), partner)
     start_above(1)
     take_wall(peers[1])
     for up in range(2, cells - 1):
@@ -533,14 +531,13 @@
 
     wait_into(second_all.at[: walls - 1], second_recv)
     share = jnp.zeros((3 * halfway, wall_count), jnp.float32)
-    for parity, tile in ((other_core, single_all.at[0, wall]), (core, single_rest)):
+    for parity, tile in ((other_core, single_all.at[0, partner]), (core, single_rest)):
         share = share + lax.dot_general(
             second_columns([second_all[2 * at + parity] for at in range(2)]),
             tile[...],
             NT,
             preferred_element_type=jnp.float32,
         )
-    own_share = jnp.zeros((halfway, LANES), jnp.float32)
     for to_cell in range(cells):
         pieces = [
             share[
@@ -551,10 +548,8 @@
         ]
         if LANES > 3 * shard_width:
             pieces.append(jnp.zeros((halfway, LANES - 3 * shard_width), jnp.float32))
-        piece = jnp.concatenate(pieces, axis=1)
-        own_share = jnp.where(cell == to_cell, piece, own_share)
-        share_out[to_cell] = piece.astype(jnp.bfloat16)
-    far_cells(lambda to_cell: to_cell < cell, lambda to_cell: share_copy(to_cell).start())
+        share_out[to_cell] = jnp.concatenate(pieces, axis=1).astype(jnp.bfloat16)
+    far_cells(lambda to_cell: to_cell <= cell, lambda to_cell: share_copy(to_cell).start())
     if cells > 2:
         start_above(cells - 1)
     far_cells(lambda to_cell: to_cell > cell, lambda to_cell: share_copy(to_cell).start())
@@ -595,6 +590,8 @@
         if step + 1 < cells:
             wait_mem(step + 1)
         left = first_columns(step)
+        if step + 1 < cells:
+            take_mem(step + 1)
         for half in range(2):
             tile = single_all[step, half * (walls // 2) : (half + 1) * (walls // 2)]
             partial[half] = partial[half] + lax.dot_general(
@@ -606,8 +603,6 @@
             if step == cells - 1:
                 part_mine[half] = partial[half]
                 exchange(half).start()
-        if step + 1 < cells:
-            take_mem(step + 1)
 
     wait_out(mem_all.at[: cells - 1], mem_send)
     wait_out(block_all, block_send)
@@ -616,7 +611,7 @@
     wait_out(second_all.at[: walls - 1], second_send)
     wait_into(data_all.at[: walls - 1], data_recv)
     wait_out(data_all.at[: walls - 1], data_send)
-    wait_out(share_in.at[: cells - 1], share_send)
+    wait_out(share_in, share_send)
 
     wait_into(lag_all.at[: cells * walls - 1], lag_recv)
 
@@ -652,10 +647,10 @@
     for i in range(3):
         out_ref[i] = total[:, i * own_points : (i + 1) * own_points]
 
-    wait_into(share_in.at[: cells - 1], share_recv)
-    second_sum = own_share
-    for step in range(1, cells):
-        second_sum = second_sum + share_in[source_at(step)].astype(jnp.float32)
+    wait_into(share_in, share_recv)
+    second_sum = jnp.zeros((halfway, LANES), jnp.float32)
+    for source in range(cells):
+        second_sum = second_sum + share_in[source].astype(jnp.float32)
     shift = lax.rem((cells - cell) * shard_width, wall_count)
     for i in range(3):
         held = pltpu.roll(data_rows[i][halfway:], shift, 1)[:, :shard_width]

time: 13.2 us -> 12.8 us (0.970)
  the two profiles are of different devices: /device:TPU:0 before, /device:TPU:29 now
where the time goes in v6:
time: 12.8 us; the launch traced here: 12.7 us
  Pallas kernels  12 us (94%)
  between operations  0.64 us (5%)
    pallas_call x1, Pallas kernels, fused_shards(): pl.pallas_call(functools.partial(fused_kernel, cells, walls), out_shape=(...  11.4 us
    pallas_call x1, Pallas kernels, fused_shards(): pl.pallas_call(write_kernel, out_shape=(jax.ShapeDtypeStruct(velocity.sha...  0.64 us

profile of v6, /device:TPU:29, one launch (start us, length us, event | category | flops | bytes accessed | tf_op | source)
XLA Modules:
  0.0 12.7 jit_solution(8467242490096021189)
XLA Ops:
  0.6 11.4 %coupling.1 = (f32[3,32,64]{2,1,0:T(8,128)S(1)}, f32[3,16,32]{2,1,0:T(8,128)S(1)}) custom-call(f32[3,256]{1,0:T(4,128)} %mem_hbm.1, bf16[3,32,64]{2,1,0:T(8,128)(2,1)} %bitcast.7, f32[3,128]{1,0:T(4,128)} %wall_hbm.1, f32[3,128]{1,0:T(4,128)} %normal_hbm.1, f32[3,32,128]{2,1,0:T(8,128)} %bitcast.6, bf16[3,16,32]{2,1,0:T(8,128)(2,1)} %bitcast.8, s32[1,32]{1,0:T(1,128)} %bitcast.9), custom_call_target="tpu_custom_call" | custom-call | tf_op jit(solution)/shard_map/coupling/pallas_call | solution.py:682
  12.0 0.6 %write.1 = (f32[3,32,64]{2,1,0:T(8,128)}, f32[3,16,32]{2,1,0:T(8,128)}) custom-call(f32[3,32,64]{2,1,0:T(8,128)S(1)} %get-tuple-element.6.velocity_ref, f32[3,16,32]{2,1,0:T(8,128)S(1)} %get-tuple-element.7.density_ref), custom_call_target="tpu_custom_call" | custom-call | tf_op jit(solution)/shard_map/write/pallas_call | solution.py:746

commit v7 on v6

--- a/solution.py
+++ b/solution.py
@@ -525,9 +525,9 @@
     take_wall(partner)
     fill_single(single_rest, mem_rows(cell, core), partner)
     start_above(1)
-    take_wall(peers[1])
     for up in range(2, cells - 1):
         start_above(up)
+    far_cells(lambda to_cell: (to_cell > cell) & (to_cell < cells - 1), start_lag)
 
     wait_into(second_all.at[: walls - 1], second_recv)
     share = jnp.zeros((3 * halfway, wall_count), jnp.float32)
@@ -550,10 +550,11 @@
             pieces.append(jnp.zeros((halfway, LANES - 3 * shard_width), jnp.float32))
         share_out[to_cell] = jnp.concatenate(pieces, axis=1).astype(jnp.bfloat16)
     far_cells(lambda to_cell: to_cell <= cell, lambda to_cell: share_copy(to_cell).start())
+    take_wall(peers[1])
     if cells > 2:
         start_above(cells - 1)
     far_cells(lambda to_cell: to_cell > cell, lambda to_cell: share_copy(to_cell).start())
-    far_cells(lambda to_cell: to_cell > cell, start_lag)
+    far_cells(lambda to_cell: (to_cell > cell) & (to_cell == cells - 1), start_lag)
     take_wall(peers[2])
 
     def source_at(step):
@@ -625,7 +626,21 @@
             for j in range(3)
             for k in range(cells)
         ]
-    lag_part = layer(jnp.concatenate(lag_row, axis=1))
+
+    moves = [
+        jnp.concatenate([scatter[:, :halfway]] * 3, axis=1),
+        jnp.concatenate([scatter[:, halfway:]] * 3, axis=1),
+    ]
+
+    def move_rows(move, rows):
+        held = []
+        for _ in range(3):
+            piece = rows.astype(jnp.bfloat16)
+            held.append(piece)
+            rows = rows - piece.astype(jnp.float32)
+        return jnp.dot(move, jnp.concatenate(held, axis=0), preferred_element_type=jnp.float32)
+
+    total = move_rows(moves[0], layer(jnp.concatenate(lag_row, axis=1)))
 
     for half in range(2):
         exchange(half).wait_recv()
@@ -638,12 +653,7 @@
             velocity = part_mine[half, held, lanes] + part_other[half, held, lanes]
             dense = 2.0 * (data_all[source, i] - velocity)
             pieces.append(dense.astype(jnp.bfloat16))
-    batched = jnp.concatenate([lag_part, layer(jnp.concatenate(pieces, axis=1))], axis=0)
-    total = jnp.zeros((columns, 3 * own_points), jnp.float32)
-    for _ in range(3):
-        piece = batched.astype(jnp.bfloat16)
-        total = total + jnp.dot(scatter, piece, preferred_element_type=jnp.float32)
-        batched = batched - piece.astype(jnp.float32)
+    total = total + move_rows(moves[1], layer(jnp.concatenate(pieces, axis=1)))
     for i in range(3):
         out_ref[i] = total[:, i * own_points : (i + 1) * own_points]
 

time: 12.8 us -> 12.7 us (level)
  the two profiles are of different devices: /device:TPU:29 before, /device:TPU:0 now
where the time goes in v7:
time: 12.7 us; the launch traced here: 12.5 us
  Pallas kernels  11.9 us (94%)
  between operations  0.64 us (5%)
    pallas_call x1, Pallas kernels, fused_shards(): pl.pallas_call(functools.partial(fused_kernel, cells, walls), out_shape=(...  11.2 us
    pallas_call x1, Pallas kernels, fused_shards(): pl.pallas_call(write_kernel, out_shape=(jax.ShapeDtypeStruct(velocity.sha...  0.64 us

profile of v7, /device:TPU:0, one launch (start us, length us, event | category | flops | bytes accessed | tf_op | source)
XLA Modules:
  0.0 12.5 jit_solution(12534136827720168232)
XLA Ops:
  0.6 11.2 %coupling.1 = (f32[3,32,64]{2,1,0:T(8,128)S(1)}, f32[3,16,32]{2,1,0:T(8,128)S(1)}) custom-call(f32[3,256]{1,0:T(4,128)} %mem_hbm.1, bf16[3,32,64]{2,1,0:T(8,128)(2,1)} %bitcast.7, f32[3,128]{1,0:T(4,128)} %wall_hbm.1, f32[3,128]{1,0:T(4,128)} %normal_hbm.1, f32[3,32,128]{2,1,0:T(8,128)} %bitcast.6, bf16[3,16,32]{2,1,0:T(8,128)(2,1)} %bitcast.8, s32[1,32]{1,0:T(1,128)} %bitcast.9), custom_call_target="tpu_custom_call" | custom-call | tf_op jit(solution)/shard_map/coupling/pallas_call | solution.py:692
  11.8 0.6 %write.1 = (f32[3,32,64]{2,1,0:T(8,128)}, f32[3,16,32]{2,1,0:T(8,128)}) custom-call(f32[3,32,64]{2,1,0:T(8,128)S(1)} %get-tuple-element.6.velocity_ref, f32[3,16,32]{2,1,0:T(8,128)S(1)} %get-tuple-element.7.density_ref), custom_call_target="tpu_custom_call" | custom-call | tf_op jit(solution)/shard_map/write/pallas_call | solution.py:756

commit v8 on v7

--- a/solution.py
+++ b/solution.py
@@ -548,7 +548,7 @@
         ]
         if LANES > 3 * shard_width:
             pieces.append(jnp.zeros((halfway, LANES - 3 * shard_width), jnp.float32))
-        share_out[to_cell] = jnp.concatenate(pieces, axis=1).astype(jnp.bfloat16)
+        share_out[to_cell] = jnp.concatenate(pieces, axis=1)
     far_cells(lambda to_cell: to_cell <= cell, lambda to_cell: share_copy(to_cell).start())
     take_wall(peers[1])
     if cells > 2:
@@ -593,6 +593,16 @@
         left = first_columns(step)
         if step + 1 < cells:
             take_mem(step + 1)
+        if step < cells - 1:
+            whole = lax.dot_general(
+                left,
+                single_all[step].reshape(2 * width, len(TILES) * LANES),
+                NT,
+                preferred_element_type=jnp.float32,
+            )
+            for half in range(2):
+                partial[half] = partial[half] + whole[:, half * width : (half + 1) * width]
+            continue
         for half in range(2):
             tile = single_all[step, half * (walls // 2) : (half + 1) * (walls // 2)]
             partial[half] = partial[half] + lax.dot_general(
@@ -660,7 +670,7 @@
     wait_into(share_in, share_recv)
     second_sum = jnp.zeros((halfway, LANES), jnp.float32)
     for source in range(cells):
-        second_sum = second_sum + share_in[source].astype(jnp.float32)
+        second_sum = second_sum + share_in[source]
     shift = lax.rem((cells - cell) * shard_width, wall_count)
     for i in range(3):
         held = pltpu.roll(data_rows[i][halfway:], shift, 1)[:, :shard_width]
@@ -718,8 +728,8 @@
             pltpu.VMEM((3 * own_points, walls * 3 * wall_count), jnp.bfloat16),
             pltpu.VMEM((2, 3 * halfway, walls // 2 * wall_count), jnp.float32),
             pltpu.VMEM((2, 3 * halfway, walls // 2 * wall_count), jnp.float32),
-            pltpu.VMEM((cells, halfway, LANES), jnp.bfloat16),
-            pltpu.VMEM((cells, halfway, LANES), jnp.bfloat16),
+            pltpu.VMEM((cells, halfway, LANES), jnp.float32),
+            pltpu.VMEM((cells, halfway, LANES), jnp.float32),
             dma((8,)),
             dma,
             dma((cells,)),

time: 12.7 us -> 12.9 us (1.016)
  the two profiles are of different devices: /device:TPU:0 before, /device:TPU:29 now
where the time goes in v8:
time: 12.9 us; the launch traced here: 12.8 us
  Pallas kernels  12.1 us (94%)
  between operations  0.64 us (5%)
    pallas_call x1, Pallas kernels, fused_shards(): pl.pallas_call(functools.partial(fused_kernel, cells, walls), out_shape=(...  11.5 us
    pallas_call x1, Pallas kernels, fused_shards(): pl.pallas_call(write_kernel, out_shape=(jax.ShapeDtypeStruct(velocity.sha...  0.64 us

profile of v8, /device:TPU:29, one launch (start us, length us, event | category | flops | bytes accessed | tf_op | source)
XLA Modules:
  0.0 12.8 jit_solution(10924070249961335845)
XLA Ops:
  0.6 11.5 %coupling.1 = (f32[3,32,64]{2,1,0:T(8,128)S(1)}, f32[3,16,32]{2,1,0:T(8,128)S(1)}) custom-call(f32[3,256]{1,0:T(4,128)} %mem_hbm.1, bf16[3,32,64]{2,1,0:T(8,128)(2,1)} %bitcast.7, f32[3,128]{1,0:T(4,128)} %wall_hbm.1, f32[3,128]{1,0:T(4,128)} %normal_hbm.1, f32[3,32,128]{2,1,0:T(8,128)} %bitcast.6, bf16[3,16,32]{2,1,0:T(8,128)(2,1)} %bitcast.8, s32[1,32]{1,0:T(1,128)} %bitcast.9), custom_call_target="tpu_custom_call" | custom-call | tf_op jit(solution)/shard_map/coupling/pallas_call | solution.py:702
  12.1 0.6 %write.1 = (f32[3,32,64]{2,1,0:T(8,128)}, f32[3,16,32]{2,1,0:T(8,128)}) custom-call(f32[3,32,64]{2,1,0:T(8,128)S(1)} %get-tuple-element.6.velocity_ref, f32[3,16,32]{2,1,0:T(8,128)S(1)} %get-tuple-element.7.density_ref), custom_call_target="tpu_custom_call" | custom-call | tf_op jit(solution)/shard_map/write/pallas_call | solution.py:766

commit v9 on v8

--- a/solution.py
+++ b/solution.py
@@ -548,7 +548,7 @@
         ]
         if LANES > 3 * shard_width:
             pieces.append(jnp.zeros((halfway, LANES - 3 * shard_width), jnp.float32))
-        share_out[to_cell] = jnp.concatenate(pieces, axis=1)
+        share_out[to_cell] = jnp.concatenate(pieces, axis=1).astype(jnp.bfloat16)
     far_cells(lambda to_cell: to_cell <= cell, lambda to_cell: share_copy(to_cell).start())
     take_wall(peers[1])
     if cells > 2:
@@ -670,7 +670,7 @@
     wait_into(share_in, share_recv)
     second_sum = jnp.zeros((halfway, LANES), jnp.float32)
     for source in range(cells):
-        second_sum = second_sum + share_in[source]
+        second_sum = second_sum + share_in[source].astype(jnp.float32)
     shift = lax.rem((cells - cell) * shard_width, wall_count)
     for i in range(3):
         held = pltpu.roll(data_rows[i][halfway:], shift, 1)[:, :shard_width]
@@ -728,8 +728,8 @@
             pltpu.VMEM((3 * own_points, walls * 3 * wall_count), jnp.bfloat16),
             pltpu.VMEM((2, 3 * halfway, walls // 2 * wall_count), jnp.float32),
             pltpu.VMEM((2, 3 * halfway, walls // 2 * wall_count), jnp.float32),
-            pltpu.VMEM((cells, halfway, LANES), jnp.float32),
-            pltpu.VMEM((cells, halfway, LANES), jnp.float32),
+            pltpu.VMEM((cells, halfway, LANES), jnp.bfloat16),
+            pltpu.VMEM((cells, halfway, LANES), jnp.bfloat16),
             dma((8,)),
             dma,
             dma((cells,)),

time: 12.9 us -> 12.7 us (0.984)
  the two profiles are of different devices: /device:TPU:29 before, /device:TPU:0 now
where the time goes in v9:
time: 12.7 us; the launch traced here: 12.5 us
  Pallas kernels  11.9 us (94%)
  between operations  0.64 us (5%)
    pallas_call x1, Pallas kernels, fused_shards(): pl.pallas_call(functools.partial(fused_kernel, cells, walls), out_shape=(...  11.2 us
    pallas_call x1, Pallas kernels, fused_shards(): pl.pallas_call(write_kernel, out_shape=(jax.ShapeDtypeStruct(velocity.sha...  0.64 us

profile of v9, /device:TPU:0, one launch (start us, length us, event | category | flops | bytes accessed | tf_op | source)
XLA Modules:
  0.0 12.5 jit_solution(1212621765902967843)
XLA Ops:
  0.6 11.2 %coupling.1 = (f32[3,32,64]{2,1,0:T(8,128)S(1)}, f32[3,16,32]{2,1,0:T(8,128)S(1)}) custom-call(f32[3,256]{1,0:T(4,128)} %mem_hbm.1, bf16[3,32,64]{2,1,0:T(8,128)(2,1)} %bitcast.7, f32[3,128]{1,0:T(4,128)} %wall_hbm.1, f32[3,128]{1,0:T(4,128)} %normal_hbm.1, f32[3,32,128]{2,1,0:T(8,128)} %bitcast.6, bf16[3,16,32]{2,1,0:T(8,128)(2,1)} %bitcast.8, s32[1,32]{1,0:T(1,128)} %bitcast.9), custom_call_target="tpu_custom_call" | custom-call | tf_op jit(solution)/shard_map/coupling/pallas_call | solution.py:702
  11.8 0.6 %write.1 = (f32[3,32,64]{2,1,0:T(8,128)}, f32[3,16,32]{2,1,0:T(8,128)}) custom-call(f32[3,32,64]{2,1,0:T(8,128)S(1)} %get-tuple-element.6.velocity_ref, f32[3,16,32]{2,1,0:T(8,128)S(1)} %get-tuple-element.7.density_ref), custom_call_target="tpu_custom_call" | custom-call | tf_op jit(solution)/shard_map/write/pallas_call | solution.py:766
